TPU v7x, 128 devices: a whole 4x4x4 slice. The times are simulated.
128 devices in a mesh: tm: 8 (over z_hi, x), space: 16 (over z_lo, y, core).
Axes of the slice: x: 4, y: 4, z: 4 (z_hi: 2, z_lo: 2; z = z_hi * 2 + z_lo), core: 2. Of those that a mesh axis runs over, the one named last changes fastest.
Arguments:
- snapshots: float32 [256, 3, 16, 32, 128], P('tm', None, 'space'), may hold values from -6 to 6
- coeffs: float32 [256, 128], replicated, may hold values from -0.375 to 0.375
- pair_table: int32 [4096, 2], replicated, may hold values from 0 to 127
Outputs:
- tensor: float32 [4096, 128], P(('tm', 'space'))
Inputs may be any that keep to these rules, and one draw needn't show every extreme that they name: `pair_table`: column 0 names the carrying mode, column 1 the carried mode.
All inputs are finite; a program needn't handle non-finite values.
Results may differ from a plain program's by a relative error of at most 0.00016.
Values sent between devices are 32-bit elements; how exact they have to be, the bound alone decides.
A program may use at most 192 MiB of HBM per device.

v0:
```python
import math

import jax
import jax.numpy as jnp
from jax import lax
from jax.sharding import PartitionSpec as P


def padded(block, sides, width):
    for axis, dim in sides:
        count = lax.axis_size(axis)
        forward = [(i, i + 1) for i in range(count - 1)]
        forward.append((count - 1, 0))
        backward = [(target, source) for source, target in forward]
        low = lax.ppermute(
            lax.slice_in_dim(block, block.shape[dim] - width, None, axis=dim), axis, forward
        )
        high = lax.ppermute(lax.slice_in_dim(block, 0, width, axis=dim), axis, backward)
        block = jnp.concatenate([low, block, high], axis=dim)
    return block


def slope_field(center, padded_x, padded_y):
    stream_slope = (padded_x[:, :, 2:] - padded_x[:, :, :-2]) * 0.5
    normal_slope = (padded_y[:, :, :, 2:] - padded_y[:, :, :, :-2]) * 0.5
    span_slope = (jnp.roll(center, -1, 4) - jnp.roll(center, 1, 4)) * 0.5
    return jnp.stack([stream_slope, normal_slope, span_slope], axis=1)


def pair_block(pair_rows, table_modes, table_slopes, flat_modes):
    modes_count = table_modes.shape[0]
    cells = flat_modes.shape[2]
    group_size = pair_rows.shape[0]
    levels = lax.broadcasted_iota(jnp.int32, (group_size, modes_count), 1)
    first_pick = (pair_rows[:, 0:1] == levels).astype(jnp.float32)
    second_pick = (pair_rows[:, 1:2] == levels).astype(jnp.float32)
    first_modes = jnp.dot(
        first_pick, table_modes, precision=lax.Precision.HIGHEST, preferred_element_type=jnp.float32
    ).reshape(group_size, 3, cells)
    second_slopes = jnp.dot(
        second_pick,
        table_slopes,
        precision=lax.Precision.HIGHEST,
        preferred_element_type=jnp.float32,
    ).reshape(group_size, 3, 3, cells)
    convection = jnp.einsum(
        "bdl,bdcl->bcl", first_modes, second_slopes, precision=lax.Precision.HIGHEST
    )
    return jnp.einsum("bcl,kcl->bk", convection, flat_modes, precision=lax.Precision.HIGHEST)


def pair_terms(pair_source, flat_modes, flat_slopes, factor, row_count):
    modes_count = flat_modes.shape[0]
    table_modes = flat_modes.reshape(modes_count, -1)
    table_slopes = flat_slopes.reshape(modes_count, -1)
    group_size = math.gcd(row_count, 64)
    grouped = pair_source.reshape(row_count // group_size, group_size, 2)

    def one_group(group_rows):
        return pair_block(group_rows, table_modes, table_slopes, flat_modes)

    result = lax.map(one_group, grouped)
    return result.reshape(row_count, -1) * factor


def shards(snapshots, coeffs, pair_table):
    mode_field = jnp.einsum(
        "sk,scxyz->kcxyz",
        coeffs,
        lax.all_to_all(snapshots, "tm", split_axis=3, concat_axis=0, tiled=True),
        precision=lax.Precision.HIGHEST,
    )
    tm_count = lax.axis_size("tm")
    space_count = lax.axis_size("space")
    total_cells = (
        mode_field.shape[2] * mode_field.shape[3] * mode_field.shape[4] * tm_count * space_count
    )
    factor = float(total_cells) ** (-0.5)
    modes_count = mode_field.shape[0]
    whole_slab = lax.all_gather(mode_field, "tm", axis=3, tiled=True)
    padded_x = padded(whole_slab, (("space", 2),), 1)
    padded_y = jnp.pad(whole_slab, ((0, 0), (0, 0), (0, 0), (1, 1), (0, 0)))
    slopes = slope_field(whole_slab, padded_x, padded_y)
    flat_modes = whole_slab.reshape(modes_count, 3, -1)
    flat_slopes = slopes.reshape(modes_count, 3, 3, -1)
    owned_count = pair_table.shape[0] // tm_count
    owned = lax.dynamic_slice_in_dim(pair_table, lax.axis_index("tm") * owned_count, owned_count, 0)
    tensor = lax.psum_scatter(
        pair_terms(
            owned,
            flat_modes,
            flat_slopes,
            factor,
            lax.axis_size("space") * (owned_count // space_count),
        ),
        "space",
        scatter_dimension=0,
        tiled=True,
    )
    return tensor


def solution(mesh):
    placed = (P("tm", None, "space", None, None), P(), P())
    return jax.shard_map(
        shards, mesh=mesh, in_specs=placed, out_specs=P(("tm", "space"), None), check_vma=False
    )
```

profile of v0, /device:TPU:6, one launch (start us, length us, event | category | flops | bytes accessed | tf_op | source)
XLA Modules:
  0.0 765.1 jit_solution(8880501986956262538)
XLA Ops:
  8.9 28.8 %all_to_all.15 = f32[32,3,1,32,128]{4,0,2,1,3:T(8,128)S(1)} all-to-all(f32[32,3,1,32,128]{4,0,2,1,3:T(8,128)S(1)} %copy.44), channel_id=1, replica_groups=mesh['tm'=8,'space'=16] {'tm'}, dimensions={3} | all-to-all | bytes 3145728 | tf_op jit(solution)/shard_map/all_to_all | solution.py:70
  40.0 86.5 %all-gather.3.cloned.1.call-done = f32[128,3,32,128]{3,0,2,1:T(8,128)} async-done(((f32[128,3,4,128]{3,0,2,1:T(8,128)}), f32[128,3,32,128]{3,0,2,1:T(8,128)}) %all-gather.3.cloned.1.call-update) | async-done | bytes 6291472 | tf_op jit(solution)/shard_map/all_gather | solution.py:80
  128.7 6.7 copy.51
  135.4 6.6 copy.55
  142.1 6.8 copy.56
  148.8 9.3 %fusion.15 = f32[128,1,3,1,32,128]{5,0,4,2,3,1:T(8,128)} fusion(f32[128,3,1,32,128]{4,0,3,1,2:T(8,128)} %bitcast.73), kind=kLoop, calls=%fused_computation.20 | loop fusion | flops 3145728 | bytes 12582912 | tf_op jit(solution)/shard_map/stack | solution.py:27
  158.2 6.6 slice_bitcast_fusion.3
  164.8 6.7 slice_bitcast_fusion.2
  171.5 10.1 %fusion.16 = f32[128,1,3,1,32,128]{5,0,4,2,3,1:T(8,128)S(1)} fusion(f32[128,1,3,1,32,1]{5,0,4,2,3,1:T(8,128)} %get-tuple-element.77, f32[128,1,3,1,32,127]{5,0,4,2,3,1:T(8,128)} %get-tuple-element.79, f32[128,1,3,1,32,127]{5,0,4,2,3,1:T(8,128)} %get-tuple-element.78, f32[128,1,3,1,32,1]{5,0,4,2,3,1:T(8,128)} %get-tuple-element.76), kind=kLoop, calls=%fused_computation.26 | loop fusion | flops 6291456 | bytes 18874368 | tf_op jit(solution)/shard_map/mul | solution.py:26
  181.6 15.2 %collective-permute-done = f32[128,3,1,32,128]{4,0,3,1,2:T(8,128)} collective-permute-done((f32[128,3,1,32,128]{4,0,3,1,2:T(8,128)}, f32[128,3,1,32,128]{4,0,3,1,2:T(8,128)}, u32[]{:S(2)}, u32[]{:S(2)}) %collective-permute-start) | collective-permute-done | bytes 6291488 | tf_op jit(solution)/shard_map/ppermute | solution.py:18
  196.8 4.0 collective-permute-done.1
  200.8 6.0 multiply_bitcast_fusion
  206.8 6.7 pad_maximum_fusion
  213.5 18.7 %copy.50 = f32[128,3,3,1,32,128]{0,5,4,2,1,3:T(8,128)} copy(f32[128,3,3,1,32,128]{5,0,4,2,3,1:T(8,128)} %pad_maximum_fusion) | data formatting | bytes 37748736 | tf_op jit(solution)/shard_map/stack | solution.py:27
  232.2 18.7 %copy.54 = f32[128,36864]{1,0:T(8,128)} copy(f32[128,36864]{0,1:T(8,128)} %bitcast.78) | data formatting | bytes 37748736 | tf_op jit(solution)/shard_map/while | solution.py:62
  250.9 447.4 %while.10 = (s32[]{:T(128)}, f32[8,64,128]{2,1,0:T(8,128)S(1)}, s32[8,64,2]{1,0,2:T(8,128)S(1)}, f32[128,36864]{1,0:T(8,128)}, f32[128,12288]{1,0:T(8,128)}, /*index=5*/f32[128,3,4096]{2,0,1:T(8,128)}, s32[]{:T(128)}) while((s32[]{:T(128)}, f32[8,64,128]{2,1,0:T(8,128)S(1)}, s32[8,64,2]{1,0,2:T(8,128)S(1)}, f32[128,36864]{1,0:T(8,128)}, ...), condition=%wide.region_1.2_spmd, body=%wide.region_0.1_spmd.sunk | while | flops 6043746304 | bytes 89164368 | solution.py:62
  250.9 13.5 %fusion.34 = f32[64,36864]{1,0:T(8,128)} fusion(f32[128,36864]{1,0:T(8,128)} %get-tuple-element.138, s32[64]{0:T(128)S(1)} %get-tuple-element.119), kind=kOutput, calls=%fused_computation.8.clone.1 | convolution fusion | flops 3623886848 | bytes 28311808 | tf_op jit(solution)/shard_map/while/body/eval_jaxpr/dot_general | solution.py:40
  264.4 12.7 %reshape.108 = f32[64,3,3,4096]{3,2,1,0:T(4,128)} reshape(f32[64,36864]{1,0:T(8,128)} %fusion.34) | data formatting | bytes 18874368 | tf_op jit(solution)/shard_map/while/body/eval_jaxpr/reshape | solution.py:45
  277.1 4.5 fusion.35
  281.6 3.7 reshape.109
  285.3 12.6 %multiply_reduce_fusion.2 = f32[64,4096,3]{1,2,0:T(4,128)S(1)} fusion(f32[64,3,3,4096]{3,2,1,0:T(4,128)} %reshape.108, f32[64,4096,3]{1,2,0:T(4,128)} %bitcast.70), kind=kLoop, calls=%fused_computation.clone.1 | loop fusion | flops 3932160 | bytes 15728640 | tf_op jit(solution)/shard_map/while
  297.9 8.9 %fusion.36 = f32[8,64,128]{2,1,0:T(8,128)S(1)} fusion(f32[8,64,128]{2,1,0:T(8,128)S(1)} %get-tuple-element.129, s32[]{:T(128)} %get-tuple-element.128, f32[128,3,4096]{2,0,1:T(8,128)} %get-tuple-element.140, f32[64,4096,3]{1,2,0:T(4,128)S(1)} %multiply_reduce_fusion.2), kind=kOutput, calls=%fused_computation.5.clone.1 | convolution fusion | flops 1207959552 | bytes 10518532 | tf_op jit(solution)/shard_map/while/body/eval_jaxpr/bcl,kcl->bk/dot_general | solution.py:49
  306.8 13.5 %fusion.34 = f32[64,36864]{1,0:T(8,128)} fusion(f32[128,36864]{1,0:T(8,128)} %get-tuple-element.138, s32[64]{0:T(128)S(1)} %get-tuple-element.119), kind=kOutput, calls=%fused_computation.8.clone.1 | convolution fusion | flops 3623886848 | bytes 28311808 | tf_op jit(solution)/shard_map/while/body/eval_jaxpr/dot_general | solution.py:40
  320.4 12.7 %reshape.108 = f32[64,3,3,4096]{3,2,1,0:T(4,128)} reshape(f32[64,36864]{1,0:T(8,128)} %fusion.34) | data formatting | bytes 18874368 | tf_op jit(solution)/shard_map/while/body/eval_jaxpr/reshape | solution.py:45
  333.0 4.5 fusion.35
  337.5 3.7 reshape.109
  341.3 12.6 %multiply_reduce_fusion.2 = f32[64,4096,3]{1,2,0:T(4,128)S(1)} fusion(f32[64,3,3,4096]{3,2,1,0:T(4,128)} %reshape.108, f32[64,4096,3]{1,2,0:T(4,128)} %bitcast.70), kind=kLoop, calls=%fused_computation.clone.1 | loop fusion | flops 3932160 | bytes 15728640 | tf_op jit(solution)/shard_map/while
  353.9 8.9 %fusion.36 = f32[8,64,128]{2,1,0:T(8,128)S(1)} fusion(f32[8,64,128]{2,1,0:T(8,128)S(1)} %get-tuple-element.129, s32[]{:T(128)} %get-tuple-element.128, f32[128,3,4096]{2,0,1:T(8,128)} %get-tuple-element.140, f32[64,4096,3]{1,2,0:T(4,128)S(1)} %multiply_reduce_fusion.2), kind=kOutput, calls=%fused_computation.5.clone.1 | convolution fusion | flops 1207959552 | bytes 10518532 | tf_op jit(solution)/shard_map/while/body/eval_jaxpr/bcl,kcl->bk/dot_general | solution.py:49
  362.8 13.5 %fusion.34 = f32[64,36864]{1,0:T(8,128)} fusion(f32[128,36864]{1,0:T(8,128)} %get-tuple-element.138, s32[64]{0:T(128)S(1)} %get-tuple-element.119), kind=kOutput, calls=%fused_computation.8.clone.1 | convolution fusion | flops 3623886848 | bytes 28311808 | tf_op jit(solution)/shard_map/while/body/eval_jaxpr/dot_general | solution.py:40
  376.3 12.7 %reshape.108 = f32[64,3,3,4096]{3,2,1,0:T(4,128)} reshape(f32[64,36864]{1,0:T(8,128)} %fusion.34) | data formatting | bytes 18874368 | tf_op jit(solution)/shard_map/while/body/eval_jaxpr/reshape | solution.py:45
  388.9 4.5 fusion.35
  393.5 3.7 reshape.109
  397.2 12.6 %multiply_reduce_fusion.2 = f32[64,4096,3]{1,2,0:T(4,128)S(1)} fusion(f32[64,3,3,4096]{3,2,1,0:T(4,128)} %reshape.108, f32[64,4096,3]{1,2,0:T(4,128)} %bitcast.70), kind=kLoop, calls=%fused_computation.clone.1 | loop fusion | flops 3932160 | bytes 15728640 | tf_op jit(solution)/shard_map/while
  409.8 8.9 %fusion.36 = f32[8,64,128]{2,1,0:T(8,128)S(1)} fusion(f32[8,64,128]{2,1,0:T(8,128)S(1)} %get-tuple-element.129, s32[]{:T(128)} %get-tuple-element.128, f32[128,3,4096]{2,0,1:T(8,128)} %get-tuple-element.140, f32[64,4096,3]{1,2,0:T(4,128)S(1)} %multiply_reduce_fusion.2), kind=kOutput, calls=%fused_computation.5.clone.1 | convolution fusion | flops 1207959552 | bytes 10518532 | tf_op jit(solution)/shard_map/while/body/eval_jaxpr/bcl,kcl->bk/dot_general | solution.py:49
  418.7 13.5 %fusion.34 = f32[64,36864]{1,0:T(8,128)} fusion(f32[128,36864]{1,0:T(8,128)} %get-tuple-element.138, s32[64]{0:T(128)S(1)} %get-tuple-element.119), kind=kOutput, calls=%fused_computation.8.clone.1 | convolution fusion | flops 3623886848 | bytes 28311808 | tf_op jit(solution)/shard_map/while/body/eval_jaxpr/dot_general | solution.py:40
  432.2 12.7 %reshape.108 = f32[64,3,3,4096]{3,2,1,0:T(4,128)} reshape(f32[64,36864]{1,0:T(8,128)} %fusion.34) | data formatting | bytes 18874368 | tf_op jit(solution)/shard_map/while/body/eval_jaxpr/reshape | solution.py:45
  444.9 4.5 fusion.35
  449.4 3.7 reshape.109
  453.1 12.6 %multiply_reduce_fusion.2 = f32[64,4096,3]{1,2,0:T(4,128)S(1)} fusion(f32[64,3,3,4096]{3,2,1,0:T(4,128)} %reshape.108, f32[64,4096,3]{1,2,0:T(4,128)} %bitcast.70), kind=kLoop, calls=%fused_computation.clone.1 | loop fusion | flops 3932160 | bytes 15728640 | tf_op jit(solution)/shard_map/while
  465.7 8.9 %fusion.36 = f32[8,64,128]{2,1,0:T(8,128)S(1)} fusion(f32[8,64,128]{2,1,0:T(8,128)S(1)} %get-tuple-element.129, s32[]{:T(128)} %get-tuple-element.128, f32[128,3,4096]{2,0,1:T(8,128)} %get-tuple-element.140, f32[64,4096,3]{1,2,0:T(4,128)S(1)} %multiply_reduce_fusion.2), kind=kOutput, calls=%fused_computation.5.clone.1 | convolution fusion | flops 1207959552 | bytes 10518532 | tf_op jit(solution)/shard_map/while/body/eval_jaxpr/bcl,kcl->bk/dot_general | solution.py:49
  474.6 13.5 %fusion.34 = f32[64,36864]{1,0:T(8,128)} fusion(f32[128,36864]{1,0:T(8,128)} %get-tuple-element.138, s32[64]{0:T(128)S(1)} %get-tuple-element.119), kind=kOutput, calls=%fused_computation.8.clone.1 | convolution fusion | flops 3623886848 | bytes 28311808 | tf_op jit(solution)/shard_map/while/body/eval_jaxpr/dot_general | solution.py:40
  488.1 12.7 %reshape.108 = f32[64,3,3,4096]{3,2,1,0:T(4,128)} reshape(f32[64,36864]{1,0:T(8,128)} %fusion.34) | data formatting | bytes 18874368 | tf_op jit(solution)/shard_map/while/body/eval_jaxpr/reshape | solution.py:45
  500.8 4.5 fusion.35
  505.3 3.7 reshape.109
  509.0 12.6 %multiply_reduce_fusion.2 = f32[64,4096,3]{1,2,0:T(4,128)S(1)} fusion(f32[64,3,3,4096]{3,2,1,0:T(4,128)} %reshape.108, f32[64,4096,3]{1,2,0:T(4,128)} %bitcast.70), kind=kLoop, calls=%fused_computation.clone.1 | loop fusion | flops 3932160 | bytes 15728640 | tf_op jit(solution)/shard_map/while
  521.6 8.9 %fusion.36 = f32[8,64,128]{2,1,0:T(8,128)S(1)} fusion(f32[8,64,128]{2,1,0:T(8,128)S(1)} %get-tuple-element.129, s32[]{:T(128)} %get-tuple-element.128, f32[128,3,4096]{2,0,1:T(8,128)} %get-tuple-element.140, f32[64,4096,3]{1,2,0:T(4,128)S(1)} %multiply_reduce_fusion.2), kind=kOutput, calls=%fused_computation.5.clone.1 | convolution fusion | flops 1207959552 | bytes 10518532 | tf_op jit(solution)/shard_map/while/body/eval_jaxpr/bcl,kcl->bk/dot_general | solution.py:49
  530.5 13.5 %fusion.34 = f32[64,36864]{1,0:T(8,128)} fusion(f32[128,36864]{1,0:T(8,128)} %get-tuple-element.138, s32[64]{0:T(128)S(1)} %get-tuple-element.119), kind=kOutput, calls=%fused_computation.8.clone.1 | convolution fusion | flops 3623886848 | bytes 28311808 | tf_op jit(solution)/shard_map/while/body/eval_jaxpr/dot_general | solution.py:40
  544.1 12.7 %reshape.108 = f32[64,3,3,4096]{3,2,1,0:T(4,128)} reshape(f32[64,36864]{1,0:T(8,128)} %fusion.34) | data formatting | bytes 18874368 | tf_op jit(solution)/shard_map/while/body/eval_jaxpr/reshape | solution.py:45
  556.7 4.5 fusion.35
  561.2 3.7 reshape.109
  565.0 12.6 %multiply_reduce_fusion.2 = f32[64,4096,3]{1,2,0:T(4,128)S(1)} fusion(f32[64,3,3,4096]{3,2,1,0:T(4,128)} %reshape.108, f32[64,4096,3]{1,2,0:T(4,128)} %bitcast.70), kind=kLoop, calls=%fused_computation.clone.1 | loop fusion | flops 3932160 | bytes 15728640 | tf_op jit(solution)/shard_map/while
  577.5 8.9 %fusion.36 = f32[8,64,128]{2,1,0:T(8,128)S(1)} fusion(f32[8,64,128]{2,1,0:T(8,128)S(1)} %get-tuple-element.129, s32[]{:T(128)} %get-tuple-element.128, f32[128,3,4096]{2,0,1:T(8,128)} %get-tuple-element.140, f32[64,4096,3]{1,2,0:T(4,128)S(1)} %multiply_reduce_fusion.2), kind=kOutput, calls=%fused_computation.5.clone.1 | convolution fusion | flops 1207959552 | bytes 10518532 | tf_op jit(solution)/shard_map/while/body/eval_jaxpr/bcl,kcl->bk/dot_general | solution.py:49
  586.5 13.5 %fusion.34 = f32[64,36864]{1,0:T(8,128)} fusion(f32[128,36864]{1,0:T(8,128)} %get-tuple-element.138, s32[64]{0:T(128)S(1)} %get-tuple-element.119), kind=kOutput, calls=%fused_computation.8.clone.1 | convolution fusion | flops 3623886848 | bytes 28311808 | tf_op jit(solution)/shard_map/while/body/eval_jaxpr/dot_general | solution.py:40
  600.0 12.7 %reshape.108 = f32[64,3,3,4096]{3,2,1,0:T(4,128)} reshape(f32[64,36864]{1,0:T(8,128)} %fusion.34) | data formatting | bytes 18874368 | tf_op jit(solution)/shard_map/while/body/eval_jaxpr/reshape | solution.py:45
  612.6 4.5 fusion.35
  617.2 3.7 reshape.109
  620.9 12.6 %multiply_reduce_fusion.2 = f32[64,4096,3]{1,2,0:T(4,128)S(1)} fusion(f32[64,3,3,4096]{3,2,1,0:T(4,128)} %reshape.108, f32[64,4096,3]{1,2,0:T(4,128)} %bitcast.70), kind=kLoop, calls=%fused_computation.clone.1 | loop fusion | flops 3932160 | bytes 15728640 | tf_op jit(solution)/shard_map/while
  633.5 8.9 %fusion.36 = f32[8,64,128]{2,1,0:T(8,128)S(1)} fusion(f32[8,64,128]{2,1,0:T(8,128)S(1)} %get-tuple-element.129, s32[]{:T(128)} %get-tuple-element.128, f32[128,3,4096]{2,0,1:T(8,128)} %get-tuple-element.140, f32[64,4096,3]{1,2,0:T(4,128)S(1)} %multiply_reduce_fusion.2), kind=kOutput, calls=%fused_computation.5.clone.1 | convolution fusion | flops 1207959552 | bytes 10518532 | tf_op jit(solution)/shard_map/while/body/eval_jaxpr/bcl,kcl->bk/dot_general | solution.py:49
  642.4 13.5 %fusion.34 = f32[64,36864]{1,0:T(8,128)} fusion(f32[128,36864]{1,0:T(8,128)} %get-tuple-element.138, s32[64]{0:T(128)S(1)} %get-tuple-element.119), kind=kOutput, calls=%fused_computation.8.clone.1 | convolution fusion | flops 3623886848 | bytes 28311808 | tf_op jit(solution)/shard_map/while/body/eval_jaxpr/dot_general | solution.py:40
  655.9 12.7 %reshape.108 = f32[64,3,3,4096]{3,2,1,0:T(4,128)} reshape(f32[64,36864]{1,0:T(8,128)} %fusion.34) | data formatting | bytes 18874368 | tf_op jit(solution)/shard_map/while/body/eval_jaxpr/reshape | solution.py:45
  668.6 4.5 fusion.35
  676.8 12.6 %multiply_reduce_fusion.2 = f32[64,4096,3]{1,2,0:T(4,128)S(1)} fusion(f32[64,3,3,4096]{3,2,1,0:T(4,128)} %reshape.108, f32[64,4096,3]{1,2,0:T(4,128)} %bitcast.70), kind=kLoop, calls=%fused_computation.clone.1 | loop fusion | flops 3932160 | bytes 15728640 | tf_op jit(solution)/shard_map/while
  689.4 8.9 %fusion.36 = f32[8,64,128]{2,1,0:T(8,128)S(1)} fusion(f32[8,64,128]{2,1,0:T(8,128)S(1)} %get-tuple-element.129, s32[]{:T(128)} %get-tuple-element.128, f32[128,3,4096]{2,0,1:T(8,128)} %get-tuple-element.140, f32[64,4096,3]{1,2,0:T(4,128)S(1)} %multiply_reduce_fusion.2), kind=kOutput, calls=%fused_computation.5.clone.1 | convolution fusion | flops 1207959552 | bytes 10518532 | tf_op jit(solution)/shard_map/while/body/eval_jaxpr/bcl,kcl->bk/dot_general | solution.py:49
  699.0 59.2 %reduce-scatter.2.cloned.1.call-done = f32[32,128]{1,0:T(8,128)} async-done(((f32[512,128]{1,0:T(8,128)}), f32[32,128]{1,0:T(8,128)}) %reduce-scatter.2.cloned.1.call-update) | async-done | bytes 16400 | tf_op jit(solution)/shard_map/reduce_scatter | solution.py:88
  (45 shorter events, 11.5 us)
Async XLA Ops:
  6.5 31.4 %copy-start = (f32[256,128]{1,0:T(8,128)S(1)}, f32[256,128]{1,0:T(8,128)}, u32[]{:S(2)}) copy-start(f32[256,128]{1,0:T(8,128)} %param.6) | copy-start | bytes 393220
  6.5 119.9 %all-gather.3.cloned.1.call-start = ((), (), s32[]{:S(2)}) async-start(), calls=%async_computation.3 | async-start | bytes 7077888 | tf_op jit(solution)/shard_map/all_gather | solution.py:80
  39.9 718.3 %reduce-scatter.2.cloned.1.call-start = ((), (), s32[]{:S(2)}) async-start(), calls=%async_computation.2 | async-start | bytes 278528 | tf_op jit(solution)/shard_map/reduce_scatter | solution.py:88
  126.4 70.4 %collective-permute-start = (f32[128,3,1,32,128]{4,0,3,1,2:T(8,128)}, f32[128,3,1,32,128]{4,0,3,1,2:T(8,128)}, u32[]{:S(2)}, u32[]{:S(2)}) collective-permute-start(f32[128,3,1,32,128]{4,0,3,1,2:T(8,128)} %bitcast.71), channel_id=1, source_target_pairs={{1,0},{2,1},{3,2},{4,3},{5,4},{6,5},{7,6},{8,7},{9,8},{10,9},{11,1... | collective-permute-start | bytes 18874376 | tf_op jit(solution)/shard_map/ppermute | solution.py:18
  128.0 72.8 %collective-permute-start.1 = (f32[128,3,1,32,128]{4,0,3,1,2:T(8,128)}, f32[128,3,1,32,128]{4,0,3,1,2:T(8,128)}, u32[]{:S(2)}, u32[]{:S(2)}) collective-permute-start(f32[128,3,1,32,128]{4,0,3,1,2:T(8,128)} %bitcast.72), channel_id=1, source_target_pairs={{0,1},{1,2},{2,3},{3,4},{4,5},{5,6},{6,7},{7,8},{8,9},{9,10},{10,1... | collective-permute-start | bytes 18874376 | tf_op jit(solution)/shard_map/ppermute | solution.py:15
  142.1 16.1 %slice-start = ((s8[6291456]{0:T(1024)(128)(4,1)}), s8[2097152]{0:T(1024)(128)(4,1)S(1)}, s32[]{:S(2)}) async-start(s8[6291456]{0:T(1024)(128)(4,1)} %bitcast.74), calls=%async_computation.4 | async-start | bytes 4194304
  148.8 9.3 %slice-start.1 = ((s8[6291456]{0:T(1024)(128)(4,1)}), s8[4194304]{0:T(1024)(128)(4,1)S(1)}, s32[]{:S(2)}) async-start(s8[6291456]{0:T(1024)(128)(4,1)} %bitcast.74), calls=%async_computation.5 | async-start | bytes 8388608
  171.5 35.3 %slice-start.2 = ((s8[6291456]{0:T(1024)(128)(4,1)}), s8[4194304]{0:T(1024)(128)(4,1)S(1)}, s32[]{:S(2)}) async-start(s8[6291456]{0:T(1024)(128)(4,1)} %bitcast.81), calls=%async_computation.6 | async-start | bytes 8388608
  171.5 35.3 %slice-start.3 = ((s8[6291456]{0:T(1024)(128)(4,1)}), s8[2097152]{0:T(1024)(128)(4,1)S(1)}, s32[]{:S(2)}) async-start(s8[6291456]{0:T(1024)(128)(4,1)} %bitcast.81), calls=%async_computation.7 | async-start | bytes 4194304
  698.3 60.0 %copy-start.1 = (f32[256,128]{1,0:T(8,128)S(1)}, f32[256,128]{1,0:T(8,128)}, u32[]{:S(2)}) copy-start(f32[256,128]{1,0:T(8,128)} %param.6) | copy-start | bytes 393220
Sparse Core Ops, SparseCore 0:
  40.0 86.3 all-gather.2
  699.1 59.0 reduce-scatter.1
where the time goes:
time: 769 us; the launch traced here: 765 us
  matrix products  217 us (28%)
  local copies, waits for them, and re-layouts  205 us (27%)
  waiting for transfers between devices  165 us (21%)
  other arithmetic  133 us (17%)
  blocking collectives  28.8 us (4%)
  between operations  13.5 us (2%)
    dot_general x8, matrix products, pair_block(): jnp.dot(second_pick, table_slopes, precision=lax.Precision.HIGHEST, prefe...  108 us
    reshape x8, local copies, waits for them, and re-layouts, pair_block(): second_slopes = jnp.dot(second_pick, table_slopes, precision=lax.Precisio...  101 us
    while x8, other arithmetic  101 us
    all_gather x1, waiting for transfers between devices, shards(): whole_slab = lax.all_gather(mode_field, 'tm', axis=3, tiled=True)  86.5 us
    dot_general x8, matrix products, pair_block(): jnp.einsum('bcl,kcl->bk', convection, flat_modes, precision=lax.Precision...  70.9 us
    reduce_scatter x1, waiting for transfers between devices, shards(): lax.psum_scatter(pair_terms(owned, flat_modes, flat_slopes, factor, lax.a...  59.2 us
    dot_general x8, matrix products, pair_block(): jnp.dot(first_pick, table_modes, precision=lax.Precision.HIGHEST, preferr...  36.1 us
    while x3, local copies, waits for them, and re-layouts, pair_terms(): result = lax.map(one_group, grouped)  32.1 us
  transfers between devices with their start and end apart: 4, of which 4 were waited for; matrix products, arithmetic and copies ran while one was open for 7% of the time, Pallas kernels for 0%

commit v1 on v0

v1 whole, which is shorter than its diff:
```python
import functools

import jax
import jax.numpy as jnp
from jax import lax
from jax.experimental import pallas as pl
from jax.experimental.pallas import tpu as pltpu
from jax.sharding import PartitionSpec as P

MESH = pl.DeviceIdType.MESH
F32 = jnp.float32
BF16 = jnp.bfloat16
MODES = 128
LANES = 128
PAIRS = 4096
STEP = 48
BLOCK = 512


def here():
    t, s = lax.axis_index("tm"), lax.axis_index("space")
    return lax.rem(t, 4), lax.rem(lax.div(s, 2), 4), lax.div(t, 4), lax.div(s, 8), lax.rem(s, 2)


def there(x, y, zh, zl, core):
    return zh * 4 + x, zl * 8 + y * 2 + core


def band_of(x, zh):
    return x + zh * (7 - 2 * x)


def owner_of(band):
    zh = lax.div(band, 4)
    return zh * 4 + band + zh * (7 - 2 * band)


def split(value):
    high = value.astype(BF16)
    return high, (value - high.astype(F32)).astype(BF16)


def dot(a, b):
    return jnp.dot(a, b, preferred_element_type=F32)


ORDER = (5, 2, 7, 4, 1, 6, 3)


def tables_kernel(
    snaps, coeffs, u_tab, s_tab, rhs, send, recv, modes, below, above, low, high,
    own_sem, a2a_s, a2a_r, x_s, x_r, y_s, y_r,
):
    x, y, zh, zl, core = here()
    tm, space = lax.axis_index("tm"), lax.axis_index("space")
    band = band_of(x, zh)
    after, before = lax.rem(space + 1, 16), lax.rem(space + 15, 16)

    def partner(rel):
        return lax.rem(zh + rel // 4, 2) * 4 + lax.rem(x + rel % 4, 4)

    barrier = pltpu.get_barrier_semaphore()
    for rel in range(1, 8):
        pl.semaphore_signal(barrier, inc=1, device_id=(partner(rel), space), device_id_type=MESH)
    for side in (after, before):
        pl.semaphore_signal(barrier, inc=1, device_id=(tm, side), device_id_type=MESH)

    for b in range(8):
        for c in range(3):
            for r in range(4):
                send[b, c * 4 + r] = snaps[pl.ds(c * 32 + 4 * b + r, 32, stride=96), :]
    own = pltpu.make_async_copy(send.at[band], recv.at[:, pl.ds(tm * 32, 32), :], own_sem)
    own.start()
    pl.semaphore_wait(barrier, 9)

    def exchange(c, rel):
        t = partner(rel)
        zt, xt = lax.div(t, 4), lax.rem(t, 4)
        return pltpu.make_async_remote_copy(
            src_ref=send.at[band_of(xt, zt), pl.ds(c * 4, 4)],
            dst_ref=recv.at[pl.ds(c * 4, 4), pl.ds(tm * 32, 32), :],
            send_sem=a2a_s.at[c, rel], recv_sem=a2a_r.at[c, rel],
            device_id=(t, space), device_id_type=MESH,
        )

    def x_copy(c, up):
        return pltpu.make_async_remote_copy(
            src_ref=modes.at[pl.ds(c * 4, 4)],
            dst_ref=(below if up else above).at[pl.ds(c * 4, 4)],
            send_sem=x_s.at[c, up], recv_sem=x_r.at[c, up],
            device_id=(tm, after if up else before), device_id_type=MESH,
        )

    def y_copy(c, up):
        target = owner_of(jnp.minimum(band + 1, 7) if up else jnp.maximum(band - 1, 0))
        return pltpu.make_async_remote_copy(
            src_ref=modes.at[c * 4 + (3 if up else 0)],
            dst_ref=(low if up else high).at[c],
            send_sem=y_s.at[c, up], recv_sem=y_r.at[c, up],
            device_id=(target, space), device_id_type=MESH,
        )

    for c in range(3):
        for rel in ORDER:
            exchange(c, rel).start()

    @pl.when(band == 0)
    def _():
        low[...] = jnp.zeros_like(low)

    @pl.when(band == 7)
    def _():
        high[...] = jnp.zeros_like(high)

    coeff_high, coeff_low = split(coeffs[...].T)
    own.wait()
    for c in range(3):
        for rel in ORDER:
            exchange(c, rel).wait_recv()
        rows = jnp.concatenate([recv[c * 4 + r] for r in range(4)], axis=1)
        row_high, row_low = split(rows)
        field = dot(coeff_high, row_high) + dot(coeff_high, row_low) + dot(coeff_low, row_high)
        for r in range(4):
            modes[c * 4 + r] = field[:, r * 128 : r * 128 + 128]
        for up in (1, 0):
            x_copy(c, up).start()

        @pl.when(band < 7)
        def _():
            y_copy(c, 1).start()

        @pl.when(band > 0)
        def _():
            y_copy(c, 0).start()

        for r in range(4):
            half, row = r // 2, r % 2
            value = field[:, r * 128 : r * 128 + 128]
            slot = half * 24 + c * 8 + row
            for copy in range(3):
                u_tab[pl.ds(slot + 2 * copy, MODES, stride=STEP), :] = value
            turned_high, turned_low = split(value.T)
            at = (half * 6 + c * 2 + row) * LANES
            rhs[at : at + LANES, 0:128] = turned_high
            rhs[at : at + LANES, 128:256] = turned_low
            slope = pltpu.roll(value, 127, 1) - pltpu.roll(value, 1, 1)
            s_tab[pl.ds(half * 24 + 16 + c * 2 + row, MODES, stride=STEP), :] = slope

    for c in range(3):
        @pl.when(band > 0)
        def _():
            y_copy(c, 1).wait_recv()

        @pl.when(band < 7)
        def _():
            y_copy(c, 0).wait_recv()

        for r in range(4):
            half, row = r // 2, r % 2
            under = low[c] if r == 0 else modes[c * 4 + r - 1]
            over = high[c] if r == 3 else modes[c * 4 + r + 1]
            s_tab[pl.ds(half * 24 + 8 + c * 2 + row, MODES, stride=STEP), :] = over - under
        for up in (1, 0):
            x_copy(c, up).wait_recv()
        for r in range(4):
            half, row = r // 2, r % 2
            slope = above[c * 4 + r] - below[c * 4 + r]
            s_tab[pl.ds(half * 24 + c * 2 + row, MODES, stride=STEP), :] = slope

    for c in range(3):
        for rel in ORDER:
            exchange(c, rel).wait_send()
        for up in (1, 0):
            x_copy(c, up).wait_send()

        @pl.when(band < 7)
        def _():
            y_copy(c, 1).wait_send()

        @pl.when(band > 0)
        def _():
            y_copy(c, 0).wait_send()


def make_tables(snaps, coeffs):
    vmem = pl.BlockSpec(memory_space=pltpu.VMEM)
    dma = pltpu.SemaphoreType.DMA
    return pl.pallas_call(
        tables_kernel,
        out_shape=[
            jax.ShapeDtypeStruct((MODES * STEP, LANES), F32),
            jax.ShapeDtypeStruct((MODES * STEP, LANES), F32),
            jax.ShapeDtypeStruct((12 * LANES, 256), BF16),
        ],
        in_specs=[vmem, vmem],
        out_specs=[vmem, vmem, vmem],
        scratch_shapes=[
            pltpu.VMEM((8, 12, 32, LANES), F32),
            pltpu.VMEM((12, 256, LANES), F32),
            pltpu.VMEM((12, MODES, LANES), F32),
            pltpu.VMEM((12, MODES, LANES), F32),
            pltpu.VMEM((12, MODES, LANES), F32),
            pltpu.VMEM((3, MODES, LANES), F32),
            pltpu.VMEM((3, MODES, LANES), F32),
            dma, dma((3, 8)), dma((3, 8)), dma((3, 2)), dma((3, 2)), dma((3, 2)), dma((3, 2)),
        ],
        compiler_params=pltpu.CompilerParams(
            collective_id=0, has_side_effects=True, vmem_limit_bytes=48 * 2**20
        ),
        name="tables",
    )(snaps, coeffs)


def pairs_kernel(factor, pairs, u_tab, s_tab, rhs, out, work):
    def block(n, _):
        def group(g, _):
            for e in range(8):
                p = n * BLOCK + g * 8 + e
                i = pl.multiple_of(pairs[2 * p] * STEP, 8)
                j = pl.multiple_of(pairs[2 * p + 1] * STEP, 8)
                for half in range(2):
                    total = None
                    for d in range(3):
                        at = half * 24 + d * 8
                        term = u_tab[pl.ds(i + at, 8), :] * s_tab[pl.ds(j + at, 8), :]
                        total = term if total is None else total + term
                    work[half, pl.ds(pl.multiple_of((g * 8 + e) * 8, 8), 8), :] = total
            return 0

        lax.fori_loop(0, BLOCK // 8, group, 0)
        highs, lows = [], []
        for half in range(2):
            for r in range(6):
                value = work[half, pl.ds(r, BLOCK, stride=8), :]
                a, b = split(value)
                highs.append(a)
                lows.append(b)
        wide = dot(jnp.concatenate(highs, axis=1), rhs[...])
        narrow = dot(jnp.concatenate(lows, axis=1), rhs[:, 0:128])
        out[pl.ds(pl.multiple_of(n * BLOCK, BLOCK), BLOCK), :] = (
            wide[:, 0:128] + (wide[:, 128:256] + narrow)
        ) * factor
        return 0

    lax.fori_loop(0, PAIRS // BLOCK, block, 0)


def pair_terms(factor, pairs, u_tab, s_tab, rhs):
    vmem = pl.BlockSpec(memory_space=pltpu.VMEM)
    return pl.pallas_call(
        functools.partial(pairs_kernel, factor),
        out_shape=jax.ShapeDtypeStruct((PAIRS, MODES), F32),
        in_specs=[pl.BlockSpec(memory_space=pltpu.SMEM), vmem, vmem, vmem],
        out_specs=vmem,
        scratch_shapes=[pltpu.VMEM((2, BLOCK * 8, LANES), F32)],
        compiler_params=pltpu.CompilerParams(vmem_limit_bytes=48 * 2**20),
        name="pairs",
    )(pairs, u_tab, s_tab, rhs)


def reduce_kernel(part, out, half, got, quarter, got_x, last, got_yz, c_s, c_r, x_s, x_r, f_s, f_r):
    x, y, zh, zl, core = here()
    tm, space = lax.axis_index("tm"), lax.axis_index("space")
    other = there(x, y, zh, zl, 1 - core)
    barrier = pltpu.get_barrier_semaphore()
    xs = [there(lax.rem(x + k, 4), y, zh, zl, core) for k in range(1, 4)]
    places = [(k % 4, (k // 4) % 2, k // 8) for k in range(16)]

    def place(k):
        dy, dl, dh = places[k]
        return lax.rem(y + dy, 4), lax.rem(zh + dh, 2), lax.rem(zl + dl, 2)

    fs = []
    for k in range(1, 16):
        ty, th, tl = place(k)
        fs.append(there(x, ty, th, tl, core))
    for target in [other, *xs, *fs]:
        pl.semaphore_signal(barrier, inc=1, device_id=target, device_id_type=MESH)
    pl.semaphore_wait(barrier, 19)

    swap = pltpu.make_async_remote_copy(
        src_ref=part.at[:, :, :, 1 - core], dst_ref=got, send_sem=c_s, recv_sem=c_r,
        device_id=other, device_id_type=MESH,
    )
    swap.start()
    swap.wait()
    for xk in range(4):
        half[xk] = part[:, xk, :, core] + got[:, xk]

    def x_copy(k):
        return pltpu.make_async_remote_copy(
            src_ref=half.at[lax.rem(x + k, 4)], dst_ref=got_x.at[k - 1],
            send_sem=x_s.at[k - 1], recv_sem=x_r.at[k - 1], device_id=xs[k - 1], device_id_type=MESH,
        )

    for k in (1, 3, 2):
        x_copy(k).start()
    for k in (1, 3, 2):
        x_copy(k).wait()
    quarter[...] = (half[x] + got_x[0]) + (got_x[1] + got_x[2])

    def f_copy(k):
        ty, th, tl = place(k)
        return pltpu.make_async_remote_copy(
            src_ref=quarter.at[th, tl * 4 + ty], dst_ref=got_yz.at[k - 1],
            send_sem=f_s.at[k - 1], recv_sem=f_r.at[k - 1], device_id=fs[k - 1], device_id_type=MESH,
        )

    for k in range(1, 16):
        f_copy(k).start()
    for k in range(1, 16):
        f_copy(k).wait()
    total = quarter[zh, zl * 4 + y]
    for k in range(15):
        total = total + got_yz[k]
    out[...] = total


def reduce_scatter(part):
    vmem = pl.BlockSpec(memory_space=pltpu.VMEM)
    dma = pltpu.SemaphoreType.DMA
    return pl.pallas_call(
        reduce_kernel,
        out_shape=jax.ShapeDtypeStruct((32, MODES), F32),
        in_specs=[vmem],
        out_specs=vmem,
        scratch_shapes=[
            pltpu.VMEM((4, 2, 8, 32, MODES), F32),
            pltpu.VMEM((2, 4, 8, 32, MODES), F32),
            pltpu.VMEM((2, 8, 32, MODES), F32),
            pltpu.VMEM((3, 2, 8, 32, MODES), F32),
            pltpu.VMEM((1, MODES), F32),
            pltpu.VMEM((15, 32, MODES), F32),
            dma, dma, dma((3,)), dma((3,)), dma((15,)), dma((15,)),
        ],
        compiler_params=pltpu.CompilerParams(
            collective_id=1, has_side_effects=True, vmem_limit_bytes=48 * 2**20
        ),
        name="reduce",
    )(part.reshape(2, 4, 8, 2, 32, MODES))


def shards(snapshots, coeffs, pair_table):
    u_tab, s_tab, rhs = make_tables(snapshots.reshape(32 * 96, LANES), coeffs)
    part = pair_terms(0.5 / 256.0, pair_table.reshape(-1), u_tab, s_tab, rhs)
    return reduce_scatter(part)


def solution(mesh):
    placed = (P("tm", None, "space", None, None), P(), P())
    return jax.shard_map(
        shards, mesh=mesh, in_specs=placed, out_specs=P(("tm", "space"), None), check_vma=False
    )
```

time: 769 us -> 98.7 us (0.13)
  matrix products: 217 us -> 0 us
  local copies, waits for them, and re-layouts: 205 us -> 6.21 us
  waiting for transfers between devices: 165 us -> 0 us
  other arithmetic: 133 us -> 0 us
  Pallas kernels: 0 us -> 92.3 us
  blocking collectives: 28.8 us -> 0 us
  between operations: 13.5 us -> 0.03 us
    dot_general x25 -> x0, matrix products: 217 us -> none  [the longest x8 108 us: pair_block(): jnp.dot(second_pick, table_slopes, precision=lax.Precision.HIGHEST, prefe...]
    reshape x17 -> x1, local copies, waits for them, and re-layouts: 131 us -> 2.73 us  [shards(): part = pair_terms(0.5 / 256.0, pair_table.reshape(-1), u_tab, s_tab, rhs)]
    while x8 -> x0, other arithmetic: 101 us -> none
    pallas_call x0 -> x3, Pallas kernels: none -> 92.3 us  [the longest x1 39.3 us: make_tables(): pl.pallas_call(tables_kernel, out_shape=[jax.ShapeDtypeStruct((MODES * ST...]
    all_gather x1 -> x0, waiting for transfers between devices: 86.5 us -> none  [shards(): whole_slab = lax.all_gather(mode_field, 'tm', axis=3, tiled=True)]
    reduce_scatter x1 -> x0, waiting for transfers between devices: 59.2 us -> none  [shards(): lax.psum_scatter(pair_terms(owned, flat_modes, flat_slopes, factor, lax.a...]
    while x3 -> x0, local copies, waits for them, and re-layouts: 32.1 us -> none  [pair_terms(): result = lax.map(one_group, grouped)]
    all_to_all x1 -> x0, blocking collectives: 28.8 us -> none  [shards(): lax.all_to_all(snapshots, 'tm', split_axis=3, concat_axis=0, tiled=True)]
  transfers between devices with their start and end apart: 4 -> 0, of which waited for: 4 -> 0; matrix products, arithmetic and copies ran while one was open for 7% -> 0% of each run, Pallas kernels for 0% -> 0%
where the time goes in v1:
time: 98.7 us; the launch traced here: 98.5 us
  Pallas kernels  92.3 us (94%)
  local copies, waits for them, and re-layouts  6.21 us (6%)
    pallas_call x1, Pallas kernels, make_tables(): pl.pallas_call(tables_kernel, out_shape=[jax.ShapeDtypeStruct((MODES * ST...  39.3 us
    pallas_call x1, Pallas kernels, reduce_scatter(): pl.pallas_call(reduce_kernel, out_shape=jax.ShapeDtypeStruct((32, MODES),...  29.3 us
    pallas_call x1, Pallas kernels, pair_terms(): pl.pallas_call(functools.partial(pairs_kernel, factor), out_shape=jax.Sha...  23.7 us
    unnamed x6, local copies, waits for them, and re-layouts  3.48 us
    reshape x1, local copies, waits for them, and re-layouts, shards(): part = pair_terms(0.5 / 256.0, pair_table.reshape(-1), u_tab, s_tab, rhs)  2.73 us

profile of v1, /device:TPU:6, one launch (start us, length us, event | category | flops | bytes accessed | tf_op | source)
XLA Modules:
  0.0 98.5 jit_solution(13441428077136468604)
XLA Ops:
  0.0 0.0 copy-start
  0.0 0.0 copy-start.1
  0.0 2.9 %copy.4 = s32[4096,2]{1,0:T(8,128)} copy(s32[4096,2]{0,1:T(2,128)} %param.5) | data formatting | bytes 65536 | tf_op args[2]
  2.9 2.7 %reshape.9.pairs = s32[8192]{0:T(1024)S(1)} reshape(s32[4096,2]{1,0:T(8,128)} %copy.4) | data formatting | bytes 65536 | tf_op jit(solution)/shard_map/reshape | solution.py:345
  5.6 0.0 copy-done
  5.6 0.0 copy-done.1
  5.6 39.3 %tables.1 = (f32[6144,128]{1,0:T(8,128)S(1)}, f32[6144,128]{1,0:T(8,128)}, bf16[1536,256]{1,0:T(8,128)(2,1)S(1)}) custom-call(f32[3072,128]{1,0:T(8,128)S(1)} %bitcast.3, f32[256,128]{1,0:T(8,128)S(1)} %copy-done.1), custom_call_target="tpu_custom_call" | custom-call | tf_op jit(solution)/shard_map/tables/pallas_call | solution.py:188
  44.9 23.7 %pairs.1 = f32[4096,128]{1,0:T(8,128)S(1)} custom-call(s32[8192]{0:T(1024)S(1)} %reshape.9.pairs, f32[6144,128]{1,0:T(8,128)S(1)} %get-tuple-element.8.u_tab, f32[6144,128]{1,0:T(8,128)} %get-tuple-element.9.s_tab, bf16[1536,256]{1,0:T(8,128)(2,1)S(1)} %get-tuple-element.10.rhs), custom_call_target="tpu_custom_call" | custom-call | tf_op jit(solution)/shard_map/pairs/pallas_call | solution.py:250
  68.7 29.3 %reduce.1 = f32[32,128]{1,0:T(8,128)S(1)} custom-call(f32[2,4,8,2,32,128]{5,4,3,2,1,0:T(8,128)S(1)} %bitcast.2), custom_call_target="tpu_custom_call" | custom-call | tf_op jit(solution)/shard_map/reduce/pallas_call | solution.py:322
  97.9 0.6 copy.6
Async XLA Ops:
  0.0 5.6 %copy-start = (f32[32,3,1,32,128]{4,3,2,1,0:T(8,128)S(1)}, f32[32,3,1,32,128]{4,3,2,1,0:T(8,128)}, u32[]{:S(2)}) copy-start(f32[32,3,1,32,128]{4,3,2,1,0:T(8,128)} %param.3) | copy-start | bytes 4718596
  0.0 5.6 %copy-start.1 = (f32[256,128]{1,0:T(8,128)S(1)}, f32[256,128]{1,0:T(8,128)}, u32[]{:S(2)}) copy-start(f32[256,128]{1,0:T(8,128)} %coeffs.1) | copy-start | bytes 393220

commit v2 on v1

--- a/solution.py
+++ b/solution.py
@@ -13,8 +13,8 @@
 MODES = 128
 LANES = 128
 PAIRS = 4096
-STEP = 48
-BLOCK = 512
+STEP = 56
+BLOCK = 128
 
 
 def here():
@@ -205,145 +205,202 @@
             dma, dma((3, 8)), dma((3, 8)), dma((3, 2)), dma((3, 2)), dma((3, 2)), dma((3, 2)),
         ],
         compiler_params=pltpu.CompilerParams(
-            collective_id=0, has_side_effects=True, vmem_limit_bytes=48 * 2**20
+            collective_id=0, has_side_effects=True, vmem_limit_bytes=24 * 2**20
         ),
         name="tables",
     )(snaps, coeffs)
 
 
-def pairs_kernel(factor, pairs, u_tab, s_tab, rhs, out, work):
-    def block(n, _):
-        def group(g, _):
-            for e in range(8):
-                p = n * BLOCK + g * 8 + e
-                i = pl.multiple_of(pairs[2 * p] * STEP, 8)
-                j = pl.multiple_of(pairs[2 * p + 1] * STEP, 8)
-                for half in range(2):
-                    total = None
-                    for d in range(3):
-                        at = half * 24 + d * 8
-                        term = u_tab[pl.ds(i + at, 8), :] * s_tab[pl.ds(j + at, 8), :]
-                        total = term if total is None else total + term
-                    work[half, pl.ds(pl.multiple_of((g * 8 + e) * 8, 8), 8), :] = total
-            return 0
-
-        lax.fori_loop(0, BLOCK // 8, group, 0)
+AXES = (0, 1, 2, 0)
+CHUNKS = 4
+PER_CHUNK = PAIRS // CHUNKS // BLOCK
+
+
+def flat(units, axis):
+    rest = [units[k] for k in range(3) if k != axis]
+    return units[axis], rest[0] * 4 + rest[1]
+
+
+def pairs_kernel(
+    factor, pairs, u_tab, s_tab, rhs, out,
+    work_a, work_b, part, got, half, got_a, quarter, got_b,
+    c_s, c_r, a_s, a_r, b_s, b_r,
+):
+    x, y, zh, zl, core = here()
+    z = zh * 2 + zl
+    barrier = pltpu.get_barrier_semaphore()
+
+    def device(tx, ty, tz, tc):
+        return there(tx, ty, lax.div(tz, 2), lax.rem(tz, 2), tc)
+
+    def moved(steps):
+        return tuple(lax.rem(a + b, 4) if b else a for a, b in zip((x, y, z), steps))
+
+    def line(axis, k):
+        return moved(tuple(k if n == axis else 0 for n in range(3)))
+
+    def plane(axis, k):
+        steps = [k // 4, k % 4]
+        return moved(tuple(0 if n == axis else steps.pop(0) for n in range(3)))
+
+    targets = [device(x, y, z, 1 - core)]
+    for axis in sorted(set(AXES)):
+        for k in range(1, 16):
+            targets.append(device(*plane(axis, k), core))
+    for n in range(len(targets)):
+        pl.semaphore_signal(barrier, inc=1, device_id=targets[n], device_id_type=MESH)
+
+    def gather(n, work):
+        q, d0 = lax.div(n, PER_CHUNK), lax.rem(n, PER_CHUNK) * (BLOCK // 8)
+        numbers = pairs.at[pl.ds(pl.multiple_of(d0 * 64 + q * 8, 8), BLOCK * 8 - 24)]
+        for e in range(BLOCK):
+            at = (e // 32) * 256 + (e // 8 % 4) * 32 + e % 8
+            i, j = numbers[at], numbers[at + 128]
+            for h in range(2):
+                total = None
+                for d in range(3):
+                    row = h * 24 + d * 8
+                    term = u_tab[i, row : row + 8, :] * s_tab[j, row : row + 8, :]
+                    total = term if total is None else total + term
+                work[(h * BLOCK + e) * 9 : (h * BLOCK + e) * 9 + 8, :] = total
+
+    def project(n, work):
         highs, lows = [], []
-        for half in range(2):
+        for h in range(2):
             for r in range(6):
-                value = work[half, pl.ds(r, BLOCK, stride=8), :]
-                a, b = split(value)
+                a, b = split(work[pl.ds(h * BLOCK * 9 + r, BLOCK, stride=9), :])
                 highs.append(a)
                 lows.append(b)
         wide = dot(jnp.concatenate(highs, axis=1), rhs[...])
         narrow = dot(jnp.concatenate(lows, axis=1), rhs[:, 0:128])
-        out[pl.ds(pl.multiple_of(n * BLOCK, BLOCK), BLOCK), :] = (
-            wide[:, 0:128] + (wide[:, 128:256] + narrow)
-        ) * factor
+        value = (wide[:, 0:128] + (wide[:, 128:256] + narrow)) * factor
+        q, d0 = lax.div(n, PER_CHUNK), lax.rem(n, PER_CHUNK) * (BLOCK // 16)
+        for u in range(BLOCK // 16):
+            for c in range(2):
+                part[q, c, d0 + u] = value[(2 * u + c) * 8 : (2 * u + c) * 8 + 8, :]
+
+    def c_copy(q):
+        return pltpu.make_async_remote_copy(
+            src_ref=part.at[q, 1 - core], dst_ref=got.at[q], send_sem=c_s.at[q], recv_sem=c_r.at[q],
+            device_id=device(x, y, z, 1 - core), device_id_type=MESH,
+        )
+
+    def a_copy(q, k):
+        to = line(AXES[q], k)
+        return pltpu.make_async_remote_copy(
+            src_ref=half.at[q, to[AXES[q]]], dst_ref=got_a.at[q, k - 1],
+            send_sem=a_s.at[q, k - 1], recv_sem=a_r.at[q, k - 1],
+            device_id=device(*to, core), device_id_type=MESH,
+        )
+
+    def b_copy(q, k):
+        to = plane(AXES[q], k)
+        return pltpu.make_async_remote_copy(
+            src_ref=quarter.at[q, flat(to, AXES[q])[1]], dst_ref=got_b.at[q, k - 1],
+            send_sem=b_s.at[q, k - 1], recv_sem=b_r.at[q, k - 1],
+            device_id=device(*to, core), device_id_type=MESH,
+        )
+
+    def stage_c(q):
+        c_copy(q).start()
+
+    def stage_a(q):
+        c_copy(q).wait_recv()
+        for u in range(64):
+            tzh, tx, tzl, ty = u // 32, (u // 8) % 4, (u // 4) % 2, u % 4
+            a, b = flat((tx, ty, tzh * 2 + tzl), AXES[q])
+            half[q, a, b] = part[q, core, u] + got[q, u]
+        for k in (1, 3, 2):
+            a_copy(q, k).start()
+
+    def stage_b(q):
+        for k in (1, 3, 2):
+            a_copy(q, k).wait_recv()
+        mine = half[q, (x, y, z)[AXES[q]]]
+        quarter[q] = (mine + got_a[q, 0]) + (got_a[q, 1] + got_a[q, 2])
+        for k in range(1, 16):
+            b_copy(q, k).start()
+
+    def stage_d(q):
+        for k in range(1, 16):
+            b_copy(q, k).wait_recv()
+        total = quarter[q, flat((x, y, z), AXES[q])[1]]
+        for k in range(15):
+            total = total + got_b[q, k]
+        out[q * 8 : q * 8 + 8, :] = total
+
+    def greet():
+        pl.semaphore_wait(barrier, len(targets))
+
+    trips = CHUNKS * PER_CHUNK
+    stages = {
+        2: [greet, (stage_c, 0)], 3: [(stage_a, 0)], 4: [(stage_c, 1)], 5: [(stage_a, 1), (stage_b, 0)],
+        6: [(stage_c, 2)], 7: [(stage_a, 2), (stage_b, 1), (stage_d, 0)],
+    }
+
+    def trip(m, _):
+        for parity, (now, later) in enumerate(((work_a, work_b), (work_b, work_a))):
+            @pl.when(lax.rem(m, 2) == parity)
+            def _():
+                gather(jnp.minimum(m + 1, trips - 1), later)
+                project(m, now)
+
+        for t, todo in stages.items():
+            @pl.when(m == t * trips // 8 - 1)
+            def _():
+                for item in todo:
+                    if callable(item):
+                        item()
+                    else:
+                        item[0](item[1])
         return 0
 
-    lax.fori_loop(0, PAIRS // BLOCK, block, 0)
+    gather(0, work_a)
+    lax.fori_loop(0, trips, trip, 0)
+    for stage, q in (
+        (stage_c, 3), (stage_b, 2), (stage_a, 3), (stage_d, 1), (stage_d, 2), (stage_b, 3), (stage_d, 3),
+    ):
+        stage(q)
+    for q in range(CHUNKS):
+        c_copy(q).wait_send()
+        for k in range(1, 4):
+            a_copy(q, k).wait_send()
+        for k in range(1, 16):
+            b_copy(q, k).wait_send()
 
 
 def pair_terms(factor, pairs, u_tab, s_tab, rhs):
     vmem = pl.BlockSpec(memory_space=pltpu.VMEM)
+    dma = pltpu.SemaphoreType.DMA
+    tile = (8, MODES)
     return pl.pallas_call(
         functools.partial(pairs_kernel, factor),
-        out_shape=jax.ShapeDtypeStruct((PAIRS, MODES), F32),
+        out_shape=jax.ShapeDtypeStruct((32, MODES), F32),
         in_specs=[pl.BlockSpec(memory_space=pltpu.SMEM), vmem, vmem, vmem],
         out_specs=vmem,
-        scratch_shapes=[pltpu.VMEM((2, BLOCK * 8, LANES), F32)],
-        compiler_params=pltpu.CompilerParams(vmem_limit_bytes=48 * 2**20),
+        scratch_shapes=[
+            pltpu.VMEM((2 * BLOCK * 9 + 8, LANES), F32),
+            pltpu.VMEM((2 * BLOCK * 9 + 8, LANES), F32),
+            pltpu.VMEM((CHUNKS, 2, 64, *tile), F32),
+            pltpu.VMEM((CHUNKS, 64, *tile), F32),
+            pltpu.VMEM((CHUNKS, 4, 16, *tile), F32),
+            pltpu.VMEM((CHUNKS, 3, 16, *tile), F32),
+            pltpu.VMEM((CHUNKS, 16, *tile), F32),
+            pltpu.VMEM((CHUNKS, 15, *tile), F32),
+            dma((CHUNKS,)), dma((CHUNKS,)), dma((CHUNKS, 3)), dma((CHUNKS, 3)),
+            dma((CHUNKS, 15)), dma((CHUNKS, 15)),
+        ],
+        compiler_params=pltpu.CompilerParams(
+            collective_id=1, has_side_effects=True, vmem_limit_bytes=24 * 2**20
+        ),
         name="pairs",
     )(pairs, u_tab, s_tab, rhs)
 
 
-def reduce_kernel(part, out, half, got, quarter, got_x, last, got_yz, c_s, c_r, x_s, x_r, f_s, f_r):
-    x, y, zh, zl, core = here()
-    tm, space = lax.axis_index("tm"), lax.axis_index("space")
-    other = there(x, y, zh, zl, 1 - core)
-    barrier = pltpu.get_barrier_semaphore()
-    xs = [there(lax.rem(x + k, 4), y, zh, zl, core) for k in range(1, 4)]
-    places = [(k % 4, (k // 4) % 2, k // 8) for k in range(16)]
-
-    def place(k):
-        dy, dl, dh = places[k]
-        return lax.rem(y + dy, 4), lax.rem(zh + dh, 2), lax.rem(zl + dl, 2)
-
-    fs = []
-    for k in range(1, 16):
-        ty, th, tl = place(k)
-        fs.append(there(x, ty, th, tl, core))
-    for target in [other, *xs, *fs]:
-        pl.semaphore_signal(barrier, inc=1, device_id=target, device_id_type=MESH)
-    pl.semaphore_wait(barrier, 19)
-
-    swap = pltpu.make_async_remote_copy(
-        src_ref=part.at[:, :, :, 1 - core], dst_ref=got, send_sem=c_s, recv_sem=c_r,
-        device_id=other, device_id_type=MESH,
-    )
-    swap.start()
-    swap.wait()
-    for xk in range(4):
-        half[xk] = part[:, xk, :, core] + got[:, xk]
-
-    def x_copy(k):
-        return pltpu.make_async_remote_copy(
-            src_ref=half.at[lax.rem(x + k, 4)], dst_ref=got_x.at[k - 1],
-            send_sem=x_s.at[k - 1], recv_sem=x_r.at[k - 1], device_id=xs[k - 1], device_id_type=MESH,
-        )
-
-    for k in (1, 3, 2):
-        x_copy(k).start()
-    for k in (1, 3, 2):
-        x_copy(k).wait()
-    quarter[...] = (half[x] + got_x[0]) + (got_x[1] + got_x[2])
-
-    def f_copy(k):
-        ty, th, tl = place(k)
-        return pltpu.make_async_remote_copy(
-            src_ref=quarter.at[th, tl * 4 + ty], dst_ref=got_yz.at[k - 1],
-            send_sem=f_s.at[k - 1], recv_sem=f_r.at[k - 1], device_id=fs[k - 1], device_id_type=MESH,
-        )
-
-    for k in range(1, 16):
-        f_copy(k).start()
-    for k in range(1, 16):
-        f_copy(k).wait()
-    total = quarter[zh, zl * 4 + y]
-    for k in range(15):
-        total = total + got_yz[k]
-    out[...] = total
-
-
-def reduce_scatter(part):
-    vmem = pl.BlockSpec(memory_space=pltpu.VMEM)
-    dma = pltpu.SemaphoreType.DMA
-    return pl.pallas_call(
-        reduce_kernel,
-        out_shape=jax.ShapeDtypeStruct((32, MODES), F32),
-        in_specs=[vmem],
-        out_specs=vmem,
-        scratch_shapes=[
-            pltpu.VMEM((4, 2, 8, 32, MODES), F32),
-            pltpu.VMEM((2, 4, 8, 32, MODES), F32),
-            pltpu.VMEM((2, 8, 32, MODES), F32),
-            pltpu.VMEM((3, 2, 8, 32, MODES), F32),
-            pltpu.VMEM((1, MODES), F32),
-            pltpu.VMEM((15, 32, MODES), F32),
-            dma, dma, dma((3,)), dma((3,)), dma((15,)), dma((15,)),
-        ],
-        compiler_params=pltpu.CompilerParams(
-            collective_id=1, has_side_effects=True, vmem_limit_bytes=48 * 2**20
-        ),
-        name="reduce",
-    )(part.reshape(2, 4, 8, 2, 32, MODES))
-
-
 def shards(snapshots, coeffs, pair_table):
     u_tab, s_tab, rhs = make_tables(snapshots.reshape(32 * 96, LANES), coeffs)
-    part = pair_terms(0.5 / 256.0, pair_table.reshape(-1), u_tab, s_tab, rhs)
-    return reduce_scatter(part)
+    u_tab, s_tab = (t.reshape(MODES, STEP, LANES) for t in (u_tab, s_tab))
+    return pair_terms(0.5 / 256.0, pair_table.reshape(32, 128, 2).transpose(0, 2, 1).reshape(-1), u_tab, s_tab, rhs)
 
 
 def solution(mesh):

time: 98.7 us -> 82.6 us (0.84)
  Pallas kernels: 92.3 us -> 78 us
  local copies, waits for them, and re-layouts: 6.21 us -> 3.67 us
    pallas_call x1 -> x0, Pallas kernels: 29.3 us -> none  [reduce_scatter(): pl.pallas_call(reduce_kernel, out_shape=jax.ShapeDtypeStruct((32, MODES),...]
    pallas_call x1, Pallas kernels: 23.7 us -> 40.7 us  [pair_terms(): pl.pallas_call(functools.partial(pairs_kernel, factor), out_shape=jax.Sha...]
    reshape x1 -> x0, local copies, waits for them, and re-layouts: 2.73 us -> none  [shards(): part = pair_terms(0.5 / 256.0, pair_table.reshape(-1), u_tab, s_tab, rhs)]
    pallas_call x1, Pallas kernels: 39.3 us -> 37.4 us  [make_tables(): pl.pallas_call(tables_kernel, out_shape=[jax.ShapeDtypeStruct((MODES * ST...]
    unnamed x6 -> x7, local copies, waits for them, and re-layouts: 3.48 us -> 3.67 us
where the time goes in v2:
time: 82.6 us; the launch traced here: 81.7 us
  Pallas kernels  78 us (94%)
  local copies, waits for them, and re-layouts  3.67 us (4%)
    pallas_call x1, Pallas kernels, pair_terms(): pl.pallas_call(functools.partial(pairs_kernel, factor), out_shape=jax.Sha...  40.7 us
    pallas_call x1, Pallas kernels, make_tables(): pl.pallas_call(tables_kernel, out_shape=[jax.ShapeDtypeStruct((MODES * ST...  37.4 us
    unnamed x7, local copies, waits for them, and re-layouts  3.67 us

profile of v2, /device:TPU:6, one launch (start us, length us, event | category | flops | bytes accessed | tf_op | source)
XLA Modules:
  0.0 81.7 jit_solution(9152336994212612468)
XLA Ops:
  0.0 0.0 copy-start
  0.0 1.4 %copy-done = f32[32,3,1,32,128]{4,3,2,1,0:T(8,128)S(1)} copy-done((f32[32,3,1,32,128]{4,3,2,1,0:T(8,128)S(1)}, f32[32,3,1,32,128]{4,3,2,1,0:T(8,128)}, u32[]{:S(2)}) %copy-start) | copy-done | bytes 1572888
  1.4 0.0 copy-start.1
  1.4 0.9 %copy-done.1 = f32[256,128]{1,0:T(8,128)S(1)} copy-done((f32[256,128]{1,0:T(8,128)S(1)}, f32[256,128]{1,0:T(8,128)}, u32[]{:S(2)}) %copy-start.1) | copy-done | bytes 131096
  2.3 37.4 %tables.1 = (f32[7168,128]{1,0:T(8,128)S(1)}, f32[7168,128]{1,0:T(8,128)S(1)}, bf16[1536,256]{1,0:T(8,128)(2,1)S(1)}) custom-call(f32[3072,128]{1,0:T(8,128)S(1)} %bitcast.10, f32[256,128]{1,0:T(8,128)S(1)} %copy-done.1), custom_call_target="tpu_custom_call" | custom-call | tf_op jit(solution)/shard_map/tables/pallas_call | solution.py:188
  39.7 0.0 copy-start.2
  39.7 0.7 copy-done.2
  40.5 40.7 %pairs.1 = f32[32,128]{1,0:T(8,128)S(1)} custom-call(s32[8192]{0:T(1024)S(1)} %bitcast.11, f32[128,56,128]{2,1,0:T(8,128)S(1)} %bitcast.8, f32[128,56,128]{2,1,0:T(8,128)S(1)} %bitcast.9, bf16[1536,256]{1,0:T(8,128)(2,1)S(1)} %get-tuple-element.10.rhs), custom_call_target="tpu_custom_call" | custom-call | tf_op jit(solution)/shard_map/pairs/pallas_call | solution.py:376
  81.1 0.6 copy.6
Async XLA Ops:
  0.0 1.4 %copy-start = (f32[32,3,1,32,128]{4,3,2,1,0:T(8,128)S(1)}, f32[32,3,1,32,128]{4,3,2,1,0:T(8,128)}, u32[]{:S(2)}) copy-start(f32[32,3,1,32,128]{4,3,2,1,0:T(8,128)} %param.3) | copy-start | bytes 4718596
  1.4 0.9 %copy-start.1 = (f32[256,128]{1,0:T(8,128)S(1)}, f32[256,128]{1,0:T(8,128)}, u32[]{:S(2)}) copy-start(f32[256,128]{1,0:T(8,128)} %coeffs.1) | copy-start | bytes 393220
  39.7 0.8 copy-start.2

commit v3 on v2

--- a/solution.py
+++ b/solution.py
@@ -211,50 +211,45 @@
     )(snaps, coeffs)
 
 
-AXES = (0, 1, 2, 0)
-CHUNKS = 4
-PER_CHUNK = PAIRS // CHUNKS // BLOCK
-
-
-def flat(units, axis):
-    rest = [units[k] for k in range(3) if k != axis]
-    return units[axis], rest[0] * 4 + rest[1]
+PIECES = 16
+FAR = 12
+CUTS = (0, 16, 36, 56, 76, 96, 128)
 
 
 def pairs_kernel(
     factor, pairs, u_tab, s_tab, rhs, out,
-    work_a, work_b, part, got, half, got_a, quarter, got_b,
-    c_s, c_r, a_s, a_r, b_s, b_r,
+    work_a, work_b, part, got, half, got_x, own, got_y, got_z,
+    c_s, c_r, x_s, x_r, y_s, y_r, z_s, z_r,
 ):
     x, y, zh, zl, core = here()
     z = zh * 2 + zl
     barrier = pltpu.get_barrier_semaphore()
 
-    def device(tx, ty, tz, tc):
-        return there(tx, ty, lax.div(tz, 2), lax.rem(tz, 2), tc)
-
-    def moved(steps):
-        return tuple(lax.rem(a + b, 4) if b else a for a, b in zip((x, y, z), steps))
-
-    def line(axis, k):
-        return moved(tuple(k if n == axis else 0 for n in range(3)))
-
-    def plane(axis, k):
-        steps = [k // 4, k % 4]
-        return moved(tuple(0 if n == axis else steps.pop(0) for n in range(3)))
-
-    targets = [device(x, y, z, 1 - core)]
-    for axis in sorted(set(AXES)):
-        for k in range(1, 16):
-            targets.append(device(*plane(axis, k), core))
-    for n in range(len(targets)):
-        pl.semaphore_signal(barrier, inc=1, device_id=targets[n], device_id_type=MESH)
-
-    def gather(n, work):
-        q, d0 = lax.div(n, PER_CHUNK), lax.rem(n, PER_CHUNK) * (BLOCK // 8)
-        numbers = pairs.at[pl.ds(pl.multiple_of(d0 * 64 + q * 8, 8), BLOCK * 8 - 24)]
-        for e in range(BLOCK):
-            at = (e // 32) * 256 + (e // 8 % 4) * 32 + e % 8
+    def device(dx=0, dy=0, dz=0, flip=0):
+        tz = lax.rem(z + dz, 4)
+        tx, ty = lax.rem(x + dx, 4), lax.rem(y + dy, 4)
+        return there(tx, ty, lax.div(tz, 2), lax.rem(tz, 2), 1 - core if flip else core)
+
+    targets = [device(flip=1)]
+    for k in range(1, 4):
+        targets += [device(dx=k), device(dy=k), device(dz=k)]
+    for target in targets:
+        pl.semaphore_signal(barrier, inc=1, device_id=target, device_id_type=MESH)
+
+    def steps(k):
+        far = k < FAR
+        r = lax.rem(k, 3)
+        dx = jnp.where(far, 1 + 2 * r - 3 * lax.div(r, 2), 0)
+        return dx, lax.rem(jnp.where(far, lax.div(k, 3), k - FAR) + 1, 4)
+
+    def gather(n, work, low, high):
+        k, wh = lax.div(n, 2), lax.rem(n, 2)
+        dx, dy = steps(k)
+        tx, ty = lax.rem(x + dx, 4), lax.rem(y + dy, 4)
+        base = (wh * 16 + tx * 4 + lax.div(ty, 2)) * 256 + lax.rem(ty, 2) * 64
+        numbers = pairs.at[pl.ds(pl.multiple_of(base, 8), 704)]
+        for e in range(low, high):
+            at = (e // 64) * 512 + e % 64
             i, j = numbers[at], numbers[at + 128]
             for h in range(2):
                 total = None
@@ -264,115 +259,109 @@
                     total = term if total is None else total + term
                 work[(h * BLOCK + e) * 9 : (h * BLOCK + e) * 9 + 8, :] = total
 
-    def project(n, work):
-        highs, lows = [], []
-        for h in range(2):
-            for r in range(6):
-                a, b = split(work[pl.ds(h * BLOCK * 9 + r, BLOCK, stride=9), :])
-                highs.append(a)
-                lows.append(b)
-        wide = dot(jnp.concatenate(highs, axis=1), rhs[...])
-        narrow = dot(jnp.concatenate(lows, axis=1), rhs[:, 0:128])
-        value = (wide[:, 0:128] + (wide[:, 128:256] + narrow)) * factor
-        q, d0 = lax.div(n, PER_CHUNK), lax.rem(n, PER_CHUNK) * (BLOCK // 16)
-        for u in range(BLOCK // 16):
+    def project(n, now, later):
+        nxt = jnp.minimum(n + 1, 2 * PIECES - 1)
+        value = None
+        for t in range(6):
+            h, r = t // 3, t % 3 * 2
+            parts = [split(now[pl.ds(h * BLOCK * 9 + r + k, BLOCK, stride=9), :]) for k in range(2)]
+            high, low = (jnp.concatenate([p[k] for p in parts], axis=1) for k in range(2))
+            wide = dot(high, rhs[t * 256 : t * 256 + 256, :])
+            narrow = dot(low, rhs[t * 256 : t * 256 + 256, 0:128])
+            term = wide[:, 0:128] + (wide[:, 128:256] + narrow)
+            value = term if value is None else value + term
+            gather(nxt, later, CUTS[t], CUTS[t + 1])
+        value = value * factor
+        k, wh = lax.div(n, 2), lax.rem(n, 2)
+        for u in range(2):
             for c in range(2):
-                part[q, c, d0 + u] = value[(2 * u + c) * 8 : (2 * u + c) * 8 + 8, :]
-
-    def c_copy(q):
-        return pltpu.make_async_remote_copy(
-            src_ref=part.at[q, 1 - core], dst_ref=got.at[q], send_sem=c_s.at[q], recv_sem=c_r.at[q],
-            device_id=device(x, y, z, 1 - core), device_id_type=MESH,
-        )
-
-    def a_copy(q, k):
-        to = line(AXES[q], k)
-        return pltpu.make_async_remote_copy(
-            src_ref=half.at[q, to[AXES[q]]], dst_ref=got_a.at[q, k - 1],
-            send_sem=a_s.at[q, k - 1], recv_sem=a_r.at[q, k - 1],
-            device_id=device(*to, core), device_id_type=MESH,
-        )
-
-    def b_copy(q, k):
-        to = plane(AXES[q], k)
-        return pltpu.make_async_remote_copy(
-            src_ref=quarter.at[q, flat(to, AXES[q])[1]], dst_ref=got_b.at[q, k - 1],
-            send_sem=b_s.at[q, k - 1], recv_sem=b_r.at[q, k - 1],
-            device_id=device(*to, core), device_id_type=MESH,
-        )
-
-    def stage_c(q):
-        c_copy(q).start()
-
-    def stage_a(q):
-        c_copy(q).wait_recv()
-        for u in range(64):
-            tzh, tx, tzl, ty = u // 32, (u // 8) % 4, (u // 4) % 2, u % 4
-            a, b = flat((tx, ty, tzh * 2 + tzl), AXES[q])
-            half[q, a, b] = part[q, core, u] + got[q, u]
-        for k in (1, 3, 2):
-            a_copy(q, k).start()
-
-    def stage_b(q):
-        for k in (1, 3, 2):
-            a_copy(q, k).wait_recv()
-        mine = half[q, (x, y, z)[AXES[q]]]
-        quarter[q] = (mine + got_a[q, 0]) + (got_a[q, 1] + got_a[q, 2])
-        for k in range(1, 16):
-            b_copy(q, k).start()
-
-    def stage_d(q):
-        for k in range(1, 16):
-            b_copy(q, k).wait_recv()
-        total = quarter[q, flat((x, y, z), AXES[q])[1]]
-        for k in range(15):
-            total = total + got_b[q, k]
-        out[q * 8 : q * 8 + 8, :] = total
-
-    def greet():
-        pl.semaphore_wait(barrier, len(targets))
-
-    trips = CHUNKS * PER_CHUNK
-    stages = {
-        2: [greet, (stage_c, 0)], 3: [(stage_a, 0)], 4: [(stage_c, 1)], 5: [(stage_a, 1), (stage_b, 0)],
-        6: [(stage_c, 2)], 7: [(stage_a, 2), (stage_b, 1), (stage_d, 0)],
-    }
+                part[k, c, wh * 2 + u] = value[(2 * u + c) * 32 : (2 * u + c) * 32 + 32, :]
+
+    def c_copy(k):
+        return pltpu.make_async_remote_copy(
+            src_ref=part.at[k, 1 - core], dst_ref=got.at[k], send_sem=c_s.at[k], recv_sem=c_r.at[k],
+            device_id=device(flip=1), device_id_type=MESH,
+        )
+
+    def x_copy(k):
+        return pltpu.make_async_remote_copy(
+            src_ref=half.at[k], dst_ref=got_x.at[k], send_sem=x_s.at[k], recv_sem=x_r.at[k],
+            device_id=device(dx=steps(k)[0]), device_id_type=MESH,
+        )
+
+    def y_copy(o):
+        return pltpu.make_async_remote_copy(
+            src_ref=own.at[o], dst_ref=got_y.at[o], send_sem=y_s.at[o], recv_sem=y_r.at[o],
+            device_id=device(dy=o + 1), device_id_type=MESH,
+        )
+
+    def z_copy(o):
+        return pltpu.make_async_remote_copy(
+            src_ref=own.at[3, lax.rem(z + o + 1, 4)], dst_ref=got_z.at[o],
+            send_sem=z_s.at[o], recv_sem=z_r.at[o], device_id=device(dz=o + 1), device_id_type=MESH,
+        )
+
+    def far_piece(k):
+        c_copy(k).wait_recv()
+        half[k] = part[k, core] + got[k]
+        x_copy(k).start()
+
+    def near_piece(o):
+        c_copy(FAR + o).wait_recv()
+        for r in range(3):
+            x_copy(3 * o + r).wait_recv()
+        total = (part[FAR + o, core] + got[FAR + o]) + (got_x[3 * o] + (got_x[3 * o + 1] + got_x[3 * o + 2]))
+        return total
 
     def trip(m, _):
         for parity, (now, later) in enumerate(((work_a, work_b), (work_b, work_a))):
             @pl.when(lax.rem(m, 2) == parity)
             def _():
-                gather(jnp.minimum(m + 1, trips - 1), later)
-                project(m, now)
-
-        for t, todo in stages.items():
-            @pl.when(m == t * trips // 8 - 1)
-            def _():
-                for item in todo:
-                    if callable(item):
-                        item()
-                    else:
-                        item[0](item[1])
+                project(m, now, later)
+
+        @pl.when(m == 1)
+        def _():
+            pl.semaphore_wait(barrier, len(targets))
+
+        k = lax.div(m, 2)
+
+        @pl.when(lax.rem(m, 2) == 1)
+        def _():
+            c_copy(k).start()
+
+        @pl.when((lax.rem(m, 2) == 1) & (k > 0) & (k <= FAR))
+        def _():
+            far_piece(k - 1)
+
         return 0
 
-    gather(0, work_a)
-    lax.fori_loop(0, trips, trip, 0)
-    for stage, q in (
-        (stage_c, 3), (stage_b, 2), (stage_a, 3), (stage_d, 1), (stage_d, 2), (stage_b, 3), (stage_d, 3),
-    ):
-        stage(q)
-    for q in range(CHUNKS):
-        c_copy(q).wait_send()
-        for k in range(1, 4):
-            a_copy(q, k).wait_send()
-        for k in range(1, 16):
-            b_copy(q, k).wait_send()
+    gather(0, work_a, 0, BLOCK)
+    lax.fori_loop(0, 2 * PIECES, trip, 0)
+    for o in range(3):
+        own[o] = near_piece(o)
+        y_copy(o).start()
+    total = near_piece(3)
+    for o in range(3):
+        y_copy(o).wait_recv()
+    own[3] = total + (got_y[0] + (got_y[1] + got_y[2]))
+    for o in (0, 2, 1):
+        z_copy(o).start()
+    for o in range(3):
+        z_copy(o).wait_recv()
+    out[...] = own[3, z] + (got_z[0] + (got_z[1] + got_z[2]))
+    for k in range(PIECES):
+        c_copy(k).wait_send()
+    for k in range(FAR):
+        x_copy(k).wait_send()
+    for o in range(3):
+        y_copy(o).wait_send()
+        z_copy(o).wait_send()
 
 
 def pair_terms(factor, pairs, u_tab, s_tab, rhs):
     vmem = pl.BlockSpec(memory_space=pltpu.VMEM)
     dma = pltpu.SemaphoreType.DMA
-    tile = (8, MODES)
+    piece = (4, 32, MODES)
     return pl.pallas_call(
         functools.partial(pairs_kernel, factor),
         out_shape=jax.ShapeDtypeStruct((32, MODES), F32),
@@ -381,14 +370,15 @@
         scratch_shapes=[
             pltpu.VMEM((2 * BLOCK * 9 + 8, LANES), F32),
             pltpu.VMEM((2 * BLOCK * 9 + 8, LANES), F32),
-            pltpu.VMEM((CHUNKS, 2, 64, *tile), F32),
-            pltpu.VMEM((CHUNKS, 64, *tile), F32),
-            pltpu.VMEM((CHUNKS, 4, 16, *tile), F32),
-            pltpu.VMEM((CHUNKS, 3, 16, *tile), F32),
-            pltpu.VMEM((CHUNKS, 16, *tile), F32),
-            pltpu.VMEM((CHUNKS, 15, *tile), F32),
-            dma((CHUNKS,)), dma((CHUNKS,)), dma((CHUNKS, 3)), dma((CHUNKS, 3)),
-            dma((CHUNKS, 15)), dma((CHUNKS, 15)),
+            pltpu.VMEM((PIECES, 2, *piece), F32),
+            pltpu.VMEM((PIECES, *piece), F32),
+            pltpu.VMEM((FAR, *piece), F32),
+            pltpu.VMEM((FAR, *piece), F32),
+            pltpu.VMEM((4, *piece), F32),
+            pltpu.VMEM((3, *piece), F32),
+            pltpu.VMEM((3, 32, MODES), F32),
+            dma((PIECES,)), dma((PIECES,)), dma((FAR,)), dma((FAR,)),
+            dma((3,)), dma((3,)), dma((3,)), dma((3,)),
         ],
         compiler_params=pltpu.CompilerParams(
             collective_id=1, has_side_effects=True, vmem_limit_bytes=24 * 2**20

time: 82.6 us -> 79.8 us (0.966)
  Pallas kernels: 78 us -> 74.8 us
    pallas_call x1, Pallas kernels: 40.7 us -> 37.5 us  [pair_terms(): pl.pallas_call(functools.partial(pairs_kernel, factor), out_shape=jax.Sha...]
where the time goes in v3:
time: 79.8 us; the launch traced here: 78.5 us
  Pallas kernels  74.8 us (94%)
  local copies, waits for them, and re-layouts  3.67 us (5%)
    pallas_call x1, Pallas kernels, pair_terms(): pl.pallas_call(functools.partial(pairs_kernel, factor), out_shape=jax.Sha...  37.5 us
    pallas_call x1, Pallas kernels, make_tables(): pl.pallas_call(tables_kernel, out_shape=[jax.ShapeDtypeStruct((MODES * ST...  37.4 us
    unnamed x7, local copies, waits for them, and re-layouts  3.67 us

profile of v3, /device:TPU:6, one launch (start us, length us, event | category | flops | bytes accessed | tf_op | source)
XLA Modules:
  0.0 78.5 jit_solution(7818186768159763407)
XLA Ops:
  0.0 0.0 copy-start
  0.0 1.4 %copy-done = f32[32,3,1,32,128]{4,3,2,1,0:T(8,128)S(1)} copy-done((f32[32,3,1,32,128]{4,3,2,1,0:T(8,128)S(1)}, f32[32,3,1,32,128]{4,3,2,1,0:T(8,128)}, u32[]{:S(2)}) %copy-start) | copy-done | bytes 1572888
  1.4 0.0 copy-start.1
  1.4 0.9 %copy-done.1 = f32[256,128]{1,0:T(8,128)S(1)} copy-done((f32[256,128]{1,0:T(8,128)S(1)}, f32[256,128]{1,0:T(8,128)}, u32[]{:S(2)}) %copy-start.1) | copy-done | bytes 131096
  2.3 37.4 %tables.1 = (f32[7168,128]{1,0:T(8,128)S(1)}, f32[7168,128]{1,0:T(8,128)S(1)}, bf16[1536,256]{1,0:T(8,128)(2,1)S(1)}) custom-call(f32[3072,128]{1,0:T(8,128)S(1)} %bitcast.10, f32[256,128]{1,0:T(8,128)S(1)} %copy-done.1), custom_call_target="tpu_custom_call" | custom-call | tf_op jit(solution)/shard_map/tables/pallas_call | solution.py:188
  39.7 0.0 copy-start.2
  39.7 0.7 copy-done.2
  40.5 37.5 %pairs.1 = f32[32,128]{1,0:T(8,128)S(1)} custom-call(s32[8192]{0:T(1024)S(1)} %bitcast.11, f32[128,56,128]{2,1,0:T(8,128)S(1)} %bitcast.8, f32[128,56,128]{2,1,0:T(8,128)S(1)} %bitcast.9, bf16[1536,256]{1,0:T(8,128)(2,1)S(1)} %get-tuple-element.10.rhs), custom_call_target="tpu_custom_call" | custom-call | tf_op jit(solution)/shard_map/pairs/pallas_call | solution.py:365
  77.9 0.6 copy.6
Async XLA Ops:
  0.0 1.4 %copy-start = (f32[32,3,1,32,128]{4,3,2,1,0:T(8,128)S(1)}, f32[32,3,1,32,128]{4,3,2,1,0:T(8,128)}, u32[]{:S(2)}) copy-start(f32[32,3,1,32,128]{4,3,2,1,0:T(8,128)} %param.3) | copy-start | bytes 4718596
  1.4 0.9 %copy-start.1 = (f32[256,128]{1,0:T(8,128)S(1)}, f32[256,128]{1,0:T(8,128)}, u32[]{:S(2)}) copy-start(f32[256,128]{1,0:T(8,128)} %coeffs.1) | copy-start | bytes 393220
  39.7 0.8 copy-start.2

commit v4 on v3

v4 whole, which is shorter than its diff:
```python
import functools

import jax
import jax.numpy as jnp
from jax import lax
from jax.experimental import pallas as pl
from jax.experimental.pallas import tpu as pltpu
from jax.sharding import PartitionSpec as P

MESH = pl.DeviceIdType.MESH
F32 = jnp.float32
BF16 = jnp.bfloat16
MODES = 128
LANES = 128
PAIRS = 4096
STEP = 56
BLOCK = 128


def here():
    t, s = lax.axis_index("tm"), lax.axis_index("space")
    return lax.rem(t, 4), lax.rem(lax.div(s, 2), 4), lax.div(t, 4), lax.div(s, 8), lax.rem(s, 2)


def there(x, y, zh, zl, core):
    return zh * 4 + x, zl * 8 + y * 2 + core


def band_of(x, zh):
    return x + zh * (7 - 2 * x)


def owner_of(band):
    zh = lax.div(band, 4)
    return zh * 4 + band + zh * (7 - 2 * band)


def split(value):
    high = value.astype(BF16)
    return high, (value - high.astype(F32)).astype(BF16)


def dot(a, b):
    return jnp.dot(a, b, preferred_element_type=F32)


ORDER = (5, 2, 7, 4, 1, 6, 3)
SPANS = ((0, 5), (5, 9), (9, 12))


def tables_kernel(
    others, snaps_hbm, coeffs_hbm, u_tab, s_tab, rhs, snaps, coeffs, send, recv, modes, below, above, low, high,
    in_sem, own_sem, a2a_s, a2a_r, x_s, x_r, y_s, y_r,
):
    x, y, zh, zl, core = here()
    tm, space = lax.axis_index("tm"), lax.axis_index("space")
    band = band_of(x, zh)
    after, before = lax.rem(space + 1, 16), lax.rem(space + 15, 16)
    loads = [
        pltpu.make_async_copy(snaps_hbm, snaps, in_sem.at[0]),
        pltpu.make_async_copy(coeffs_hbm, coeffs, in_sem.at[1]),
    ]
    for load in loads:
        load.start()

    def partner(rel):
        return lax.rem(zh + rel // 4, 2) * 4 + lax.rem(x + rel % 4, 4)

    barrier = pltpu.get_barrier_semaphore()
    for rel in range(1, 8):
        pl.semaphore_signal(barrier, inc=1, device_id=(partner(rel), space), device_id_type=MESH)
    for side in (after, before):
        pl.semaphore_signal(barrier, inc=1, device_id=(tm, side), device_id_type=MESH)
    for target in others:
        pl.semaphore_signal(barrier, inc=1, device_id=target, device_id_type=MESH)

    loads[0].wait()
    for b in range(8):
        for c in range(3):
            for r in range(4):
                send[b, c * 4 + r] = snaps[pl.ds(c * 32 + 4 * b + r, 32, stride=96), :]
    own = pltpu.make_async_copy(send.at[band], recv.at[:, pl.ds(tm * 32, 32), :], own_sem)
    own.start()
    pl.semaphore_wait(barrier, 9 + len(others))

    def exchange(g, rel):
        first, last = SPANS[g]
        t = partner(rel)
        zt, xt = lax.div(t, 4), lax.rem(t, 4)
        return pltpu.make_async_remote_copy(
            src_ref=send.at[band_of(xt, zt), pl.ds(first, last - first)],
            dst_ref=recv.at[pl.ds(first, last - first), pl.ds(tm * 32, 32), :],
            send_sem=a2a_s.at[g, rel], recv_sem=a2a_r.at[g, rel],
            device_id=(t, space), device_id_type=MESH,
        )

    def x_copy(g, up):
        first, last = SPANS[g]
        return pltpu.make_async_remote_copy(
            src_ref=modes.at[pl.ds(first, last - first)],
            dst_ref=(below if up else above).at[pl.ds(first, last - first)],
            send_sem=x_s.at[g, up], recv_sem=x_r.at[g, up],
            device_id=(tm, after if up else before), device_id_type=MESH,
        )

    def y_copy(c, up):
        target = owner_of(jnp.minimum(band + 1, 7) if up else jnp.maximum(band - 1, 0))
        return pltpu.make_async_remote_copy(
            src_ref=modes.at[c * 4 + (3 if up else 0)],
            dst_ref=(low if up else high).at[c],
            send_sem=y_s.at[c, up], recv_sem=y_r.at[c, up],
            device_id=(target, space), device_id_type=MESH,
        )

    for g in range(len(SPANS)):
        for rel in ORDER:
            exchange(g, rel).start()

    @pl.when(band == 0)
    def _():
        low[...] = jnp.zeros_like(low)

    @pl.when(band == 7)
    def _():
        high[...] = jnp.zeros_like(high)

    loads[1].wait()
    coeff_high, coeff_low = split(coeffs[...].T)
    own.wait()

    def place(row):
        c, r = row // 4, row % 4
        return c, r, r // 2 * 24 + r % 2

    for g, (first, last) in enumerate(SPANS):
        for rel in ORDER:
            exchange(g, rel).wait_recv()
        rows = jnp.concatenate([recv[row] for row in range(first, last)], axis=1)
        row_high, row_low = split(rows)
        field = dot(coeff_high, row_high) + dot(coeff_high, row_low) + dot(coeff_low, row_high)
        for row in range(first, last):
            modes[row] = field[:, (row - first) * 128 : (row - first) * 128 + 128]
        for up in (1, 0):
            x_copy(g, up).start()
        for row in range(first, last):
            c, r, _ = place(row)
            if r == 3:
                @pl.when(band < 7)
                def _():
                    y_copy(c, 1).start()
            if r == 0:
                @pl.when(band > 0)
                def _():
                    y_copy(c, 0).start()

        for row in range(first, last):
            c, r, slot = place(row)
            value = field[:, (row - first) * 128 : (row - first) * 128 + 128]
            for copy in range(3):
                u_tab[pl.ds(slot + c * 8 + 2 * copy, MODES, stride=STEP), :] = value
            turned_high, turned_low = split(value.T)
            at = (r // 2 * 6 + c * 2 + r % 2) * LANES
            rhs[at : at + LANES, 0:128] = turned_high
            rhs[at : at + LANES, 128:256] = turned_low
            slope = pltpu.roll(value, 127, 1) - pltpu.roll(value, 1, 1)
            s_tab[pl.ds(slot + 16 + c * 2, MODES, stride=STEP), :] = slope

    for row in range(12):
        c, r, slot = place(row)
        if r in (1, 2):
            s_tab[pl.ds(slot + 8 + c * 2, MODES, stride=STEP), :] = modes[row + 1] - modes[row - 1]
    for g, (first, last) in enumerate(SPANS):
        for row in range(first, last):
            c, r, slot = place(row)
            if r == 0:
                @pl.when(band > 0)
                def _():
                    y_copy(c, 1).wait_recv()
                s_tab[pl.ds(slot + 8 + c * 2, MODES, stride=STEP), :] = modes[row + 1] - low[c]
            if r == 3:
                @pl.when(band < 7)
                def _():
                    y_copy(c, 0).wait_recv()
                s_tab[pl.ds(slot + 8 + c * 2, MODES, stride=STEP), :] = high[c] - modes[row - 1]
        for up in (1, 0):
            x_copy(g, up).wait_recv()
        for row in range(first, last):
            c, r, slot = place(row)
            s_tab[pl.ds(slot + c * 2, MODES, stride=STEP), :] = above[row] - below[row]

    for c in range(3):
        for rel in ORDER:
            exchange(c, rel).wait_send()
        for up in (1, 0):
            x_copy(c, up).wait_send()

        @pl.when(band < 7)
        def _():
            y_copy(c, 1).wait_send()

        @pl.when(band > 0)
        def _():
            y_copy(c, 0).wait_send()


def device(dx=0, dy=0, dz=0, flip=0):
    x, y, zh, zl, core = here()
    tz = lax.rem(zh * 2 + zl + dz, 4)
    tx, ty = lax.rem(x + dx, 4), lax.rem(y + dy, 4)
    return there(tx, ty, lax.div(tz, 2), lax.rem(tz, 2), 1 - core if flip else core)


PIECES = 16
FAR = 12
CUTS = (0, 16, 36, 56, 76, 96, 128)


def pairs_kernel(
    factor, pairs, u_tab, s_tab, rhs, out,
    work_a, work_b, part, got, half, got_x, own, got_y, got_z,
    c_s, c_r, x_s, x_r, y_s, y_r, z_s, z_r,
):
    x, y, zh, zl, core = here()
    z = zh * 2 + zl

    def steps(k):
        far = k < FAR
        r = lax.rem(k, 3)
        dx = jnp.where(far, 1 + 2 * r - 3 * lax.div(r, 2), 0)
        return dx, lax.rem(jnp.where(far, lax.div(k, 3), k - FAR) + 1, 4)

    def gather(n, work, low, high):
        k, wh = lax.div(n, 2), lax.rem(n, 2)
        dx, dy = steps(k)
        tx, ty = lax.rem(x + dx, 4), lax.rem(y + dy, 4)
        base = (wh * 16 + tx * 4 + lax.div(ty, 2)) * 256 + lax.rem(ty, 2) * 64
        numbers = pairs.at[pl.ds(pl.multiple_of(base, 8), 704)]
        for e in range(low, high):
            at = (e // 64) * 512 + e % 64
            i, j = numbers[at], numbers[at + 128]
            for h in range(2):
                total = None
                for d in range(3):
                    row = h * 24 + d * 8
                    term = u_tab[i, row : row + 8, :] * s_tab[j, row : row + 8, :]
                    total = term if total is None else total + term
                work[(h * BLOCK + e) * 9 : (h * BLOCK + e) * 9 + 8, :] = total

    def project(n, now, later):
        nxt = jnp.minimum(n + 1, 2 * PIECES - 1)
        value = None
        for t in range(6):
            h, r = t // 3, t % 3 * 2
            parts = [split(now[pl.ds(h * BLOCK * 9 + r + k, BLOCK, stride=9), :]) for k in range(2)]
            high, low = (jnp.concatenate([p[k] for p in parts], axis=1) for k in range(2))
            wide = dot(high, rhs[t * 256 : t * 256 + 256, :])
            narrow = dot(low, rhs[t * 256 : t * 256 + 256, 0:128])
            term = wide[:, 0:128] + (wide[:, 128:256] + narrow)
            value = term if value is None else value + term
            gather(nxt, later, CUTS[t], CUTS[t + 1])
        value = value * factor
        k, wh = lax.div(n, 2), lax.rem(n, 2)
        for u in range(2):
            for c in range(2):
                part[k, c, wh * 2 + u] = value[(2 * u + c) * 32 : (2 * u + c) * 32 + 32, :]

    def c_copy(k):
        return pltpu.make_async_remote_copy(
            src_ref=part.at[k, 1 - core], dst_ref=got.at[k], send_sem=c_s.at[k], recv_sem=c_r.at[k],
            device_id=device(flip=1), device_id_type=MESH,
        )

    def x_copy(k):
        return pltpu.make_async_remote_copy(
            src_ref=half.at[k], dst_ref=got_x.at[k], send_sem=x_s.at[k], recv_sem=x_r.at[k],
            device_id=device(dx=steps(k)[0]), device_id_type=MESH,
        )

    def y_copy(o):
        return pltpu.make_async_remote_copy(
            src_ref=own.at[o], dst_ref=got_y.at[o], send_sem=y_s.at[o], recv_sem=y_r.at[o],
            device_id=device(dy=o + 1), device_id_type=MESH,
        )

    def z_copy(o):
        return pltpu.make_async_remote_copy(
            src_ref=own.at[3, lax.rem(z + o + 1, 4)], dst_ref=got_z.at[o],
            send_sem=z_s.at[o], recv_sem=z_r.at[o], device_id=device(dz=o + 1), device_id_type=MESH,
        )

    def far_piece(k):
        c_copy(k).wait_recv()
        half[k] = part[k, core] + got[k]
        x_copy(k).start()

    def near_piece(o):
        c_copy(FAR + o).wait_recv()
        for r in range(3):
            x_copy(3 * o + r).wait_recv()
        own[o] = (part[FAR + o, core] + got[FAR + o]) + (got_x[3 * o] + (got_x[3 * o + 1] + got_x[3 * o + 2]))
        if o < 3:
            y_copy(o).start()

    def trip(m, _):
        for parity, (now, later) in enumerate(((work_a, work_b), (work_b, work_a))):
            @pl.when(lax.rem(m, 2) == parity)
            def _():
                project(m, now, later)

        k = lax.div(m, 2)

        @pl.when(lax.rem(m, 2) == 1)
        def _():
            c_copy(k).start()

        @pl.when((lax.rem(m, 2) == 1) & (k > 1) & (k < FAR + 2))
        def _():
            far_piece(k - 2)

        for o in range(2):
            @pl.when(m == 2 * FAR + 4 + 2 * o)
            def _():
                near_piece(o)

        return 0

    gather(0, work_a, 0, BLOCK)
    lax.fori_loop(0, 2 * PIECES, trip, 0)
    near_piece(2)
    near_piece(3)
    for o in range(3):
        y_copy(o).wait_recv()
    own[3] = own[3] + (got_y[0] + (got_y[1] + got_y[2]))
    for o in (0, 2, 1):
        z_copy(o).start()
    for o in range(3):
        z_copy(o).wait_recv()
    out[...] = own[3, z] + (got_z[0] + (got_z[1] + got_z[2]))
    for k in range(PIECES):
        c_copy(k).wait_send()
    for k in range(FAR):
        x_copy(k).wait_send()
    for o in range(3):
        y_copy(o).wait_send()
        z_copy(o).wait_send()


def whole_kernel(factor, pairs_hbm, snaps_hbm, coeffs_hbm, out, *scratch):
    pairs, pairs_sem, u_tab, s_tab, rhs, *rest = scratch
    first, second = rest[:17], rest[17:]
    load = pltpu.make_async_copy(pairs_hbm, pairs, pairs_sem)
    load.start()
    others = [device(flip=1)]
    for k in range(1, 4):
        others += [device(dx=k), device(dy=k), device(dz=k)]
    tables_kernel(others, snaps_hbm, coeffs_hbm, u_tab, s_tab, rhs, *first)
    load.wait()
    u_tab, s_tab = (tab.reshape(MODES, STEP, LANES) for tab in (u_tab, s_tab))
    pairs_kernel(factor, pairs, u_tab, s_tab, rhs, out, *second)


def shards(snapshots, coeffs, pair_table):
    dma = pltpu.SemaphoreType.DMA
    piece = (4, 32, MODES)
    hbm = pl.BlockSpec(memory_space=pltpu.HBM)
    return pl.pallas_call(
        functools.partial(whole_kernel, 0.5 / 256.0),
        out_shape=jax.ShapeDtypeStruct((32, MODES), F32),
        in_specs=[hbm, hbm, hbm],
        out_specs=pl.BlockSpec(memory_space=pltpu.VMEM),
        scratch_shapes=[
            pltpu.SMEM((2 * PAIRS,), jnp.int32),
            dma,
            pltpu.VMEM((MODES * STEP, LANES), F32),
            pltpu.VMEM((MODES * STEP, LANES), F32),
            pltpu.VMEM((12 * LANES, 256), BF16),
            pltpu.VMEM((32 * 96, LANES), F32),
            pltpu.VMEM((256, MODES), F32),
            pltpu.VMEM((8, 12, 32, LANES), F32),
            pltpu.VMEM((12, 256, LANES), F32),
            pltpu.VMEM((12, MODES, LANES), F32),
            pltpu.VMEM((12, MODES, LANES), F32),
            pltpu.VMEM((12, MODES, LANES), F32),
            pltpu.VMEM((3, MODES, LANES), F32),
            pltpu.VMEM((3, MODES, LANES), F32),
            dma((2,)), dma, dma((3, 8)), dma((3, 8)), dma((3, 2)), dma((3, 2)), dma((3, 2)), dma((3, 2)),
            pltpu.VMEM((2 * BLOCK * 9 + 8, LANES), F32),
            pltpu.VMEM((2 * BLOCK * 9 + 8, LANES), F32),
            pltpu.VMEM((PIECES, 2, *piece), F32),
            pltpu.VMEM((PIECES, *piece), F32),
            pltpu.VMEM((FAR, *piece), F32),
            pltpu.VMEM((FAR, *piece), F32),
            pltpu.VMEM((4, *piece), F32),
            pltpu.VMEM((3, *piece), F32),
            pltpu.VMEM((3, 32, MODES), F32),
            dma((PIECES,)), dma((PIECES,)), dma((FAR,)), dma((FAR,)),
            dma((3,)), dma((3,)), dma((3,)), dma((3,)),
        ],
        compiler_params=pltpu.CompilerParams(
            collective_id=0, has_side_effects=True, vmem_limit_bytes=60 * 2**20
        ),
        name="whole",
    )(
        pair_table.reshape(32, 128, 2).transpose(0, 2, 1).reshape(-1),
        snapshots.reshape(32 * 96, LANES),
        coeffs,
    )


def solution(mesh):
    placed = (P("tm", None, "space", None, None), P(), P())
    return jax.shard_map(
        shards, mesh=mesh, in_specs=placed, out_specs=P(("tm", "space"), None), check_vma=False
    )
```

time: 79.8 us -> 75.6 us (0.947)
  local copies, waits for them, and re-layouts: 3.67 us -> 1.32 us
  Pallas kernels: 74.8 us -> 72.8 us
    unnamed x7 -> x1, local copies, waits for them, and re-layouts: 3.67 us -> 1.32 us
    pallas_call x2 -> x1, Pallas kernels: 74.8 us -> 72.8 us  [shards(): pl.pallas_call(functools.partial(whole_kernel, 0.5 / 256.0), out_shape=ja...]
where the time goes in v4:
time: 75.6 us; the launch traced here: 74.1 us
  Pallas kernels  72.8 us (96%)
  local copies, waits for them, and re-layouts  1.32 us (2%)
    pallas_call x1, Pallas kernels, shards(): pl.pallas_call(functools.partial(whole_kernel, 0.5 / 256.0), out_shape=ja...  72.8 us

profile of v4, /device:TPU:6, one launch (start us, length us, event | category | flops | bytes accessed | tf_op | source)
XLA Modules:
  0.0 74.1 jit_solution(7988196164856499666)
XLA Ops:
  0.0 72.8 %whole.1 = f32[32,128]{1,0:T(8,128)} custom-call(s32[8192]{0:T(1024)} %bitcast.7, f32[3072,128]{1,0:T(8,128)} %bitcast.6, f32[256,128]{1,0:T(8,128)} %coeffs_hbm.1), custom_call_target="tpu_custom_call" | custom-call | tf_op jit(solution)/shard_map/whole/pallas_call | solution.py:366
  72.8 1.3 %copy.6 = f32[32,128]{1,0:T(8,128)} copy(f32[32,128]{1,0:T(8,128)} %whole.1) | data formatting | bytes 32768

commit v5 on v4

--- a/solution.py
+++ b/solution.py
@@ -153,17 +153,17 @@
                 def _():
                     y_copy(c, 0).start()
 
-        for row in range(first, last):
-            c, r, slot = place(row)
-            value = field[:, (row - first) * 128 : (row - first) * 128 + 128]
-            for copy in range(3):
-                u_tab[pl.ds(slot + c * 8 + 2 * copy, MODES, stride=STEP), :] = value
-            turned_high, turned_low = split(value.T)
-            at = (r // 2 * 6 + c * 2 + r % 2) * LANES
-            rhs[at : at + LANES, 0:128] = turned_high
-            rhs[at : at + LANES, 128:256] = turned_low
-            slope = pltpu.roll(value, 127, 1) - pltpu.roll(value, 1, 1)
-            s_tab[pl.ds(slot + 16 + c * 2, MODES, stride=STEP), :] = slope
+    for row in range(12):
+        c, r, slot = place(row)
+        value = modes[row]
+        for copy in range(3):
+            u_tab[pl.ds(slot + c * 8 + 2 * copy, MODES, stride=STEP), :] = value
+        turned_high, turned_low = split(value.T)
+        at = (r // 2 * 6 + c * 2 + r % 2) * LANES
+        rhs[at : at + LANES, 0:128] = turned_high
+        rhs[at : at + LANES, 128:256] = turned_low
+        slope = pltpu.roll(value, 127, 1) - pltpu.roll(value, 1, 1)
+        s_tab[pl.ds(slot + 16 + c * 2, MODES, stride=STEP), :] = slope
 
     for row in range(12):
         c, r, slot = place(row)
@@ -217,8 +217,8 @@
 
 def pairs_kernel(
     factor, pairs, u_tab, s_tab, rhs, out,
-    work_a, work_b, part, got, half, got_x, own, got_y, got_z,
-    c_s, c_r, x_s, x_r, y_s, y_r, z_s, z_r,
+    work_a, work_b, part, got, half, got_x, own, got_f,
+    c_s, c_r, x_s, x_r, f_s, f_r,
 ):
     x, y, zh, zl, core = here()
     z = zh * 2 + zl
@@ -276,16 +276,11 @@
             device_id=device(dx=steps(k)[0]), device_id_type=MESH,
         )
 
-    def y_copy(o):
-        return pltpu.make_async_remote_copy(
-            src_ref=own.at[o], dst_ref=got_y.at[o], send_sem=y_s.at[o], recv_sem=y_r.at[o],
-            device_id=device(dy=o + 1), device_id_type=MESH,
-        )
-
-    def z_copy(o):
-        return pltpu.make_async_remote_copy(
-            src_ref=own.at[3, lax.rem(z + o + 1, 4)], dst_ref=got_z.at[o],
-            send_sem=z_s.at[o], recv_sem=z_r.at[o], device_id=device(dz=o + 1), device_id_type=MESH,
+    def f_copy(o, dz):
+        return pltpu.make_async_remote_copy(
+            src_ref=own.at[o, lax.rem(z + dz, 4)], dst_ref=got_f.at[o, dz],
+            send_sem=f_s.at[o, dz], recv_sem=f_r.at[o, dz],
+            device_id=device(dy=(o + 1) % 4, dz=dz), device_id_type=MESH,
         )
 
     def far_piece(k):
@@ -298,8 +293,9 @@
         for r in range(3):
             x_copy(3 * o + r).wait_recv()
         own[o] = (part[FAR + o, core] + got[FAR + o]) + (got_x[3 * o] + (got_x[3 * o + 1] + got_x[3 * o + 2]))
-        if o < 3:
-            y_copy(o).start()
+        for dz in (2, 1, 3, 0):
+            if o < 3 or dz:
+                f_copy(o, dz).start()
 
     def trip(m, _):
         for parity, (now, later) in enumerate(((work_a, work_b), (work_b, work_a))):
@@ -328,21 +324,21 @@
     lax.fori_loop(0, 2 * PIECES, trip, 0)
     near_piece(2)
     near_piece(3)
-    for o in range(3):
-        y_copy(o).wait_recv()
-    own[3] = own[3] + (got_y[0] + (got_y[1] + got_y[2]))
-    for o in (0, 2, 1):
-        z_copy(o).start()
-    for o in range(3):
-        z_copy(o).wait_recv()
-    out[...] = own[3, z] + (got_z[0] + (got_z[1] + got_z[2]))
+    total = own[3, z]
+    for o in range(4):
+        for dz in range(4):
+            if o < 3 or dz:
+                f_copy(o, dz).wait_recv()
+                total = total + got_f[o, dz]
+    out[...] = total
     for k in range(PIECES):
         c_copy(k).wait_send()
     for k in range(FAR):
         x_copy(k).wait_send()
-    for o in range(3):
-        y_copy(o).wait_send()
-        z_copy(o).wait_send()
+    for o in range(4):
+        for dz in range(4):
+            if o < 3 or dz:
+                f_copy(o, dz).wait_send()
 
 
 def whole_kernel(factor, pairs_hbm, snaps_hbm, coeffs_hbm, out, *scratch):
@@ -351,8 +347,8 @@
     load = pltpu.make_async_copy(pairs_hbm, pairs, pairs_sem)
     load.start()
     others = [device(flip=1)]
-    for k in range(1, 4):
-        others += [device(dx=k), device(dy=k), device(dz=k)]
+    others += [device(dx=k) for k in range(1, 4)]
+    others += [device(dy=k // 4, dz=k % 4) for k in range(1, 16)]
     tables_kernel(others, snaps_hbm, coeffs_hbm, u_tab, s_tab, rhs, *first)
     load.wait()
     u_tab, s_tab = (tab.reshape(MODES, STEP, LANES) for tab in (u_tab, s_tab))
@@ -391,10 +387,8 @@
             pltpu.VMEM((FAR, *piece), F32),
             pltpu.VMEM((FAR, *piece), F32),
             pltpu.VMEM((4, *piece), F32),
-            pltpu.VMEM((3, *piece), F32),
-            pltpu.VMEM((3, 32, MODES), F32),
-            dma((PIECES,)), dma((PIECES,)), dma((FAR,)), dma((FAR,)),
-            dma((3,)), dma((3,)), dma((3,)), dma((3,)),
+            pltpu.VMEM((4, *piece), F32),
+            dma((PIECES,)), dma((PIECES,)), dma((FAR,)), dma((FAR,)), dma((4, 4)), dma((4, 4)),
         ],
         compiler_params=pltpu.CompilerParams(
             collective_id=0, has_side_effects=True, vmem_limit_bytes=60 * 2**20

time: 75.6 us -> 71.3 us (0.943); the launches traced: 74.1 us -> 70.8 us
  Pallas kernels: 72.8 us -> 69.5 us
    pallas_call x1, Pallas kernels: 72.8 us -> 69.5 us  [shards(): pl.pallas_call(functools.partial(whole_kernel, 0.5 / 256.0), out_shape=ja...]
where the time goes in v5:
time: 71.3 us; the launch traced here: 70.8 us
  Pallas kernels  69.5 us (97%)
  local copies, waits for them, and re-layouts  1.32 us (2%)
    pallas_call x1, Pallas kernels, shards(): pl.pallas_call(functools.partial(whole_kernel, 0.5 / 256.0), out_shape=ja...  69.5 us

profile of v5, /device:TPU:6, one launch (start us, length us, event | category | flops | bytes accessed | tf_op | source)
XLA Modules:
  0.0 70.8 jit_solution(3718283674255334936)
XLA Ops:
  0.0 69.5 %whole.1 = f32[32,128]{1,0:T(8,128)} custom-call(s32[8192]{0:T(1024)} %bitcast.7, f32[3072,128]{1,0:T(8,128)} %bitcast.6, f32[256,128]{1,0:T(8,128)} %coeffs_hbm.1), custom_call_target="tpu_custom_call" | custom-call | tf_op jit(solution)/shard_map/whole/pallas_call | solution.py:362
  69.5 1.3 %copy.6 = f32[32,128]{1,0:T(8,128)} copy(f32[32,128]{1,0:T(8,128)} %whole.1) | data formatting | bytes 32768

commit v6 on v5

--- a/solution.py
+++ b/solution.py
@@ -75,14 +75,6 @@
         pl.semaphore_signal(barrier, inc=1, device_id=target, device_id_type=MESH)
 
     loads[0].wait()
-    for b in range(8):
-        for c in range(3):
-            for r in range(4):
-                send[b, c * 4 + r] = snaps[pl.ds(c * 32 + 4 * b + r, 32, stride=96), :]
-    own = pltpu.make_async_copy(send.at[band], recv.at[:, pl.ds(tm * 32, 32), :], own_sem)
-    own.start()
-    pl.semaphore_wait(barrier, 9 + len(others))
-
     def exchange(g, rel):
         first, last = SPANS[g]
         t = partner(rel)
@@ -112,9 +104,16 @@
             device_id=(target, space), device_id_type=MESH,
         )
 
-    for g in range(len(SPANS)):
+    for g, (first, last) in enumerate(SPANS):
+        for row in range(first, last):
+            for b in range(8):
+                send[b, row] = snaps[pl.ds(row // 4 * 32 + 4 * b + row % 4, 32, stride=96), :]
+        if g == 0:
+            pl.semaphore_wait(barrier, 9 + len(others))
         for rel in ORDER:
             exchange(g, rel).start()
+    own = pltpu.make_async_copy(send.at[band], recv.at[:, pl.ds(tm * 32, 32), :], own_sem)
+    own.start()
 
     @pl.when(band == 0)
     def _():
@@ -140,8 +139,16 @@
         field = dot(coeff_high, row_high) + dot(coeff_high, row_low) + dot(coeff_low, row_high)
         for row in range(first, last):
             modes[row] = field[:, (row - first) * 128 : (row - first) * 128 + 128]
-        for up in (1, 0):
-            x_copy(g, up).start()
+        for up, crossing in ((1, y * 2 + core == 7), (0, y * 2 + core == 0)):
+            @pl.when(jnp.logical_not(crossing))
+            def _():
+                x_copy(g, up).start()
+
+            if g > 0:
+                @pl.when(crossing)
+                def _():
+                    for late in range(g * 2 - 2, g + 1):
+                        x_copy(late, up).start()
         for row in range(first, last):
             c, r, _ = place(row)
             if r == 3:
@@ -212,7 +219,7 @@
 
 PIECES = 16
 FAR = 12
-CUTS = (0, 16, 36, 56, 76, 96, 128)
+CUTS = (0, 12, 28, 46, 66, 92, 128)
 
 
 def pairs_kernel(

time: 71.3 us -> 70.8 us (level)
  Pallas kernels: 69.5 us -> 68.6 us
    pallas_call x1, Pallas kernels: 69.5 us -> 68.6 us  [shards(): pl.pallas_call(functools.partial(whole_kernel, 0.5 / 256.0), out_shape=ja...]
where the time goes in v6:
time: 70.8 us; the launch traced here: 69.9 us
  Pallas kernels  68.6 us (97%)
  local copies, waits for them, and re-layouts  1.32 us (2%)
    pallas_call x1, Pallas kernels, shards(): pl.pallas_call(functools.partial(whole_kernel, 0.5 / 256.0), out_shape=ja...  68.6 us

profile of v6, /device:TPU:6, one launch (start us, length us, event | category | flops | bytes accessed | tf_op | source)
XLA Modules:
  0.0 69.9 jit_solution(17388868128243949632)
XLA Ops:
  0.0 68.6 %whole.1 = f32[32,128]{1,0:T(8,128)} custom-call(s32[8192]{0:T(1024)} %bitcast.7, f32[3072,128]{1,0:T(8,128)} %bitcast.6, f32[256,128]{1,0:T(8,128)} %coeffs_hbm.1), custom_call_target="tpu_custom_call" | custom-call | tf_op jit(solution)/shard_map/whole/pallas_call | solution.py:369
  68.6 1.3 %copy.6 = f32[32,128]{1,0:T(8,128)} copy(f32[32,128]{1,0:T(8,128)} %whole.1) | data formatting | bytes 32768
